TPU v7x, 256 devices: a whole 4x4x8 slice. The times are simulated.
256 devices in a mesh: lat: 4 (over y), lon: 64 (over z, x, core).
Axes of the slice: x: 4, y: 4, z: 8, core: 2. Of those that a mesh axis runs over, the one named last changes fastest.
Arguments:
- field: float32 [64, 16384, 128], P('lat', 'lon'), may hold values from -6 to 6
- ocean: int32 [64, 16384], P('lat', 'lon'), may hold values 0 or 1
- modes: int32 [128], replicated, may hold values from 1 to 8191, as said below
- spectral_weight: float32 [128, 2, 128, 128], P('lon'), may hold values from -0.375 to 0.375
- local_weight: float32 [128, 128], replicated, may hold values from -0.5 to 0.5
- layer_bias: float32 [128], replicated, may hold values from -4 to 4
- conv_weight: float32 [3, 3, 128, 128], replicated, may hold values from -0.1875 to 0.1875
- conv_bias: float32 [128], replicated, may hold values from -2 to 2
Outputs:
- decoded: float32 [64, 16384, 128], P('lat', 'lon')
Inputs may be any that keep to these rules, and one draw needn't show every extreme that they name: `modes`: distinct wavenumbers.
All inputs are finite; a program needn't handle non-finite values. No bound on the sum of `ocean` on one device may be relied on, other than what follows from the above.
Results may differ from a plain program's by a relative error of at most 0.0001.
Values sent between devices are 32-bit elements; how exact they have to be, the bound alone decides.
A program may use at most 64 MiB of HBM per device.

v0:
```python
import functools
import math

import jax
import jax.numpy as jnp
from jax import lax
from jax.experimental import pallas as pl
from jax.experimental.pallas import tpu as pltpu
from jax.sharding import Mesh
from jax.sharding import PartitionSpec as P

LON = ("lon_0", "lon_1", "lon_2")
HIGH = lax.Precision.HIGHEST
PAD = 8
BF = jnp.bfloat16
F32 = jnp.float32


def split_up(value, dim, size):
    dims = value.shape
    blocks = value.reshape(*dims[:dim], size, dims[dim] // size, *dims[dim + 1 :])
    return jnp.moveaxis(blocks, dim, 0)


def sent_and_summed(value, axis, dim):
    size = lax.axis_size(axis)
    blocks = lax.all_to_all(split_up(value, dim, size), axis, 0, 0, tiled=True)
    return jnp.sum(blocks, axis=0)


def sum_by_axis(value, axes, dim):
    far, near = axes
    own = sent_and_summed(split_up(value, dim, lax.axis_size(far)), near, dim + 1)
    return jnp.sum(lax.all_to_all(own, far, 0, 0, tiled=True), axis=0)


def sent_to_all(value, axis):
    copies = jnp.broadcast_to(value, (lax.axis_size(axis), *value.shape))
    return lax.all_to_all(copies, axis, split_axis=0, concat_axis=0, tiled=True)


def joined_along(blocks, dim):
    blocks = jnp.moveaxis(blocks, 0, dim)
    dims = blocks.shape
    return blocks.reshape(*dims[:dim], dims[dim] * dims[dim + 1], *dims[dim + 2 :])


def whole_of(value, axes, dim):
    far, near = axes
    blocks = sent_to_all(sent_to_all(value, far), near)
    return joined_along(blocks.swapaxes(0, 1).reshape(-1, *value.shape), dim)


def with_halo(block, sides, width, periodic):
    for axis, dim in sides:
        count = lax.axis_size(axis)
        forward = [(i, i + 1) for i in range(count - 1)]
        if periodic:
            forward.append((count - 1, 0))
        backward = [(target, source) for source, target in forward]
        low = lax.ppermute(
            lax.slice_in_dim(block, block.shape[dim] - width, None, axis=dim), axis, forward
        )
        high = lax.ppermute(lax.slice_in_dim(block, 0, width, axis=dim), axis, backward)
        block = jnp.concatenate([low, block, high], axis=dim)
    return block


def mix_modes(coeffs, weights):
    w_real = weights[:, 0]
    w_imag = weights[:, 1]
    upper = jnp.concatenate([w_real, w_imag], -1)
    lower = jnp.concatenate([-w_imag, w_real], -1)
    blocks = jnp.concatenate([upper, lower], 1)
    return jnp.einsum("mic,mcd->mid", coeffs, blocks, precision=HIGH)


def halves(value):
    high = value.astype(BF)
    return high, (value - high.astype(F32)).astype(BF)


def stored_halves(value):
    high = lax.reduce_precision(value, 8, 7)
    return high.astype(BF), (value - high).astype(BF)


def dot(a, b):
    return jnp.dot(a, b, preferred_element_type=F32)


def lane_sum(acc):
    return acc[:, :128] + acc[:, 128:]


def tail_kernel(
    rows, width, scale, lat_axis, lat_count,
    mixed_hbm, field_hbm, wet_ref, table_ref, local_ref, bias_ref, conv_ref, conv_bias_ref,
    out_hbm,
    mixed, field, hidden, mask, taps, local, out, sem_in, sem_out,
):
    ext = rows + 2
    wide = width + 2 * PAD
    half = rows // 2

    def mixed_copy(r):
        part, block = (1, half) if r == 0 else (0, half) if r == ext - 1 else divmod(r - 1, half)
        source = mixed_hbm.at[part, :, pl.ds(block * 128, 128)]
        return pltpu.make_async_copy(source, mixed.at[r], sem_in.at[0, r])

    def field_copy(r):
        return pltpu.make_async_copy(field_hbm.at[r], field.at[r], sem_in.at[1, r])

    for r in range(ext):
        mixed_copy(r).start()
        field_copy(r).start()

    high, low = halves(local_ref[...])
    both = jnp.concatenate([high, low], 1)
    local[0:128] = both
    local[128:256] = both
    for a in range(3):
        for b in range(3):
            high, low = halves(conv_ref[a, b])
            both = jnp.concatenate([high, low], 1)
            for q in range(2):
                taps[pl.ds(a * 256 + q * 128, 128), pl.ds(b * 256, 256)] = both

    lane = lax.broadcasted_iota(jnp.int32, (wide, 128), 1)
    lat = lax.axis_index(lat_axis)
    above = jnp.where(lat > 0, 1.0, 0.0).astype(F32)
    below = jnp.where(lat < lat_count - 1, 1.0, 0.0).astype(F32)
    top = pltpu.roll(wet_ref[0], 128 - rows, 1) * above
    bottom = pltpu.roll(wet_ref[2], rows, 1) * below
    wet = jnp.where(lane == 0, top, jnp.where(lane == rows + 1, bottom, wet_ref[1])).astype(BF)

    @pl.loop(0, ext)
    def _(r):
        pltpu.make_async_copy(field_hbm.at[0], field.at[0], sem_in.at[1, r]).wait()
        pltpu.make_async_copy(
            mixed_hbm.at[0, :, pl.ds(0, 128)], mixed.at[0], sem_in.at[0, r]
        ).wait()
        high, low = halves(mixed[r])
        both = jnp.concatenate([high, low], 1)
        spectral = lane_sum(dot(table_ref[...], jnp.concatenate([both, both], 0))) * scale
        high, low = halves(field[r])
        point = lane_sum(dot(jnp.concatenate([high, low], 1), local[...]))
        pick = lax.broadcasted_iota(jnp.int32, (128, 128), 0) == r
        cover = dot(wet, pick.astype(F32).astype(BF))
        mask[r] = cover
        value = cover * jax.nn.gelu(spectral + point + bias_ref[...], approximate=True)
        high, low = halves(value)
        both = jnp.concatenate([high, low], 1)
        for a in range(3):
            hidden[r + 2 - a, :, pl.ds(a * 256, 256)] = both

    group = 2

    @pl.loop(0, rows // group)
    def _(t):
        i = t * group
        block = hidden[pl.ds(i + 2, group)].reshape(group * wide, 768)
        left, middle, right = (
            lane_sum(dot(block, taps[:, pl.ds(b * 256, 256)])) for b in range(3)
        )
        total = pltpu.roll(left, 1, 0) + middle + pltpu.roll(right, group * wide - 1, 0)
        total = (total + conv_bias_ref[...]).reshape(group, wide, 128)
        total = total * mask[pl.ds(i + 1, group)]
        out[pl.ds(i, group)] = total[:, PAD : PAD + width]
        pltpu.make_async_copy(
            out.at[pl.ds(i, group)], out_hbm.at[pl.ds(i, group)], sem_out.at[t]
        ).start()

    @pl.loop(0, rows // group)
    def _(t):
        pltpu.make_async_copy(
            out.at[pl.ds(0, group)], out_hbm.at[pl.ds(0, group)], sem_out.at[t]
        ).wait()


def tail(mixed, field, wet, table, local_weight, layer_bias, conv_weight, conv_bias, rows, width, scale, lat_axis, lat_count):
    ext = rows + 2
    wide = width + 2 * PAD
    vmem = pl.BlockSpec(memory_space=pltpu.VMEM)
    hbm = pl.BlockSpec(memory_space=pl.ANY)
    return pl.pallas_call(
        functools.partial(tail_kernel, rows, width, scale, lat_axis, lat_count),
        out_shape=jax.ShapeDtypeStruct((rows, width, 128), F32),
        in_specs=[hbm, hbm] + [vmem] * 6,
        out_specs=hbm,
        scratch_shapes=[
            pltpu.VMEM((ext, 256, 128), F32),
            pltpu.VMEM((ext, wide, 128), F32),
            pltpu.VMEM((rows + 4, wide, 768), BF),
            pltpu.VMEM((ext, wide, 128), F32),
            pltpu.VMEM((768, 768), BF),
            pltpu.VMEM((256, 256), BF),
            pltpu.VMEM((rows, width, 128), F32),
            pltpu.SemaphoreType.DMA((2, ext)),
            pltpu.SemaphoreType.DMA((rows // 2,)),
        ],
        compiler_params=pltpu.CompilerParams(vmem_limit_bytes=40 << 20),
        name="tail",
    )(mixed, field, wet, table, local_weight, layer_bias.reshape(1, 128), conv_weight, conv_bias.reshape(1, 128))


def table_of(lon_ids, modes_of, parity, total_lon):
    phase = (modes_of * lon_ids + parity * (total_lon // 4)) % total_lon
    return jnp.cos(phase.astype(F32) * (2.0 * math.pi / total_lon))


def per_device(field, ocean, modes, spectral_weight, local_weight, layer_bias, conv_weight, conv_bias):
    rows, width, channels = field.shape
    lon_count = lax.axis_size(LON)
    total_lon = width * lon_count
    total_modes = modes.shape[0]
    lon_start = lax.axis_index(LON) * width
    scale = 2.0 / math.sqrt(total_modes)
    pair = jnp.repeat(modes, 2)
    parity = jnp.arange(2 * total_modes, dtype=jnp.int32) % 2
    lon_ids = (lon_start - PAD + jnp.arange(width + 2 * PAD, dtype=jnp.int32) + total_lon) % total_lon
    inverse = jnp.concatenate(stored_halves(table_of(lon_ids[:, None], pair[None], parity[None], total_lon)), 1)
    own_ids = lon_start + jnp.arange(width, dtype=jnp.int32)
    forward = table_of(own_ids[None], pair[:, None], parity[:, None], total_lon)
    partial = jnp.einsum("kj,ijc->kic", forward, field, precision=HIGH) / math.sqrt(total_lon)
    partial = partial.reshape(total_modes, 2, rows, channels).swapaxes(1, 2).reshape(total_modes, rows, 2 * channels)
    own_coeffs = sum_by_axis(partial, (("lon_0", "lon_1"), "lon_2"), 0)
    own_mixed = mix_modes(own_coeffs, spectral_weight)
    own_mixed = with_halo(own_mixed, (("lat", 1),), 1, False)
    mixed = whole_of(own_mixed, (("lon_0", "lon_1"), "lon_2"), 0)
    mixed = mixed.reshape(total_modes, rows + 2, 2, channels).swapaxes(1, 2)
    mixed = mixed.reshape(2 * total_modes, (rows + 2) * channels)
    half = rows // 2 * channels
    last = rows * channels + channels
    parts = jnp.stack([
        jnp.concatenate([mixed[:, channels : channels + half], mixed[:, last:]], 1),
        jnp.concatenate([mixed[:, channels + half : last], mixed[:, :channels]], 1),
    ])
    gap = ((0, 0), (PAD - 1, PAD - 1), (0, 0))
    edged = with_halo(field, (("lat", 0),), 1, False)
    edged = jnp.pad(with_halo(edged, ((LON, 1),), 1, True), gap)
    wet = with_halo(ocean.astype(F32)[:, :, None], (("lat", 0),), 1, False)
    wet = with_halo(wet, ((LON, 1),), 1, True)
    wet = jnp.pad(wet, gap)[:, :, 0].T
    mid = jnp.pad(wet, ((0, 0), (0, 128 - rows - 2)))
    above = jnp.pad(wet[:, :1], ((0, 0), (rows, 127 - rows)))
    below = jnp.pad(wet[:, rows + 1 :], ((0, 0), (1, 126)))
    return tail(
        parts, edged, jnp.stack([above, mid, below]), inverse, local_weight, layer_bias,
        conv_weight, conv_bias, rows, width, scale, "lat", lax.axis_size("lat"),
    )


def solution(mesh):
    split = Mesh(mesh.devices.reshape(mesh.shape["lat"], 8, 4, 2), ("lat", "lon_0", "lon_1", "lon_2"))
    placed = (P("lat", LON, None), P("lat", LON), P(), P(LON, None, None, None), P(), P(), P(), P())
    return jax.shard_map(
        per_device, mesh=split, in_specs=placed, out_specs=P("lat", LON, None), check_vma=False
    )
```

profile of v0, /device:TPU:1, one launch (start us, length us, event | category | flops | bytes accessed | tf_op | source)
XLA Modules:
  0.0 154.8 jit_solution(5561030969298449352)
XLA Ops:
  0.9 4.5 %convolution_multiply_fusion = f32[256,16,128]{2,0,1:T(8,128)S(1)} fusion(f32[16,256,128]{2,1,0:T(8,128)} %param.8, s32[256]{0:T(256)S(1)} %get-tuple-element.25, s32[256]{0:T(256)S(1)} %get-tuple-element.26, s32[256]{0:T(256)S(1)} %mul.69), kind=kOutput, calls=%fused_computation.8 | convolution fusion | flops 1612120064 | bytes 4197376 | tf_op jit(solution)/shard_map/kj,ijc->kic/dot_general | solution.py:225
  5.4 1.2 copy.58
  6.6 2.7 %reshape_reshape_reshape.6 = f32[32,2,2,16,256]{4,3,2,1,0:T(8,128)} reshape(f32[128,16,2,128]{3,2,1,0:T(2,128)S(1)} %bitcast.56) | data formatting | bytes 4194304 | tf_op jit(solution)/shard_map/reshape;reshape;reshape | solution.py:21
  9.3 3.2 %copy.36 = f32[2,32,2,16,256]{4,2,1,3,0:T(2,128)S(1)} copy(f32[2,32,2,16,256]{4,3,2,0,1:T(8,128)} %bitcast.57) | data formatting | bytes 4194304 | tf_op jit(solution)/shard_map/transpose | solution.py:22
  12.5 8.2 %all_to_all.20 = f32[2,32,2,16,256]{4,2,1,3,0:T(2,128)S(1)} all-to-all(f32[2,32,2,16,256]{4,2,1,3,0:T(2,128)S(1)} %copy.36), channel_id=1, replica_groups=mesh['lat'=4,'lon_0'=8,'lon_1'=4,'lon_2'=2] {'lon_2'}, dimensions={0} | all-to-all | bytes 4194304 | tf_op jit(solution)/shard_map/all_to_all | solution.py:27
  20.7 2.0 %reduce_sum.18 = f32[32,2,16,256]{3,1,0,2:T(2,128)S(1)} reduce(f32[2,32,2,16,256]{4,2,1,3,0:T(2,128)S(1)} %all_to_all.20, f32[]{:T(128)} %constant.79.clone.1), dimensions={0}, to_apply=%region_0.1 | reduce | flops 262144 | bytes 3145732 | tf_op jit(solution)/shard_map/reduce_sum | solution.py:28
  22.8 1.6 %copy.38 = f32[32,2,16,256]{3,1,2,0:T(2,128)} copy(f32[32,2,16,256]{3,1,0,2:T(2,128)S(1)} %reduce_sum.18) | data formatting | bytes 2097152 | tf_op jit(solution)/shard_map/reduce_sum | solution.py:28
  24.3 9.3 %all-to-all-start.1 = ((f32[32,2,16,256]{3,1,2,0:T(2,128)}), f32[32,2,16,256]{3,1,2,0:T(2,128)S(1)}, u32[]{:S(2)}, u32[]{:S(2)}) async-start(f32[32,2,16,256]{3,1,2,0:T(2,128)} %copy.38), calls=%async_computation.1 | async-start | bytes 2097152 | tf_op jit(solution)/shard_map/all_to_all | solution.py:34
  34.4 3.9 %collective-permute-start.2 = (f32[1,256,128]{2,1,0:T(8,128)}, f32[1,256,128]{2,1,0:T(8,128)}, u32[]{:S(2)}, u32[]{:S(2)}) collective-permute-start(f32[1,256,128]{2,1,0:T(8,128)} %get-tuple-element.12), channel_id=1, source_target_pairs={{0,64},{64,128},{128,192},{1,65},{65,129},{129,193},{2,66},{66,130... | collective-permute-start | bytes 393224 | tf_op jit(solution)/shard_map/ppermute | solution.py:61
  38.3 1.3 collective-permute-start.3
  40.9 4.6 %collective-permute-start.6 = (f32[1,256,1]{1,2,0:T(1,128)}, f32[1,256,1]{1,2,0:T(1,128)}, u32[]{:S(2)}, u32[]{:S(2)}) collective-permute-start(f32[1,256,1]{1,2,0:T(1,128)} %get-tuple-element.22), channel_id=1, source_target_pairs={{0,64},{64,128},{128,192},{1,65},{65,129},{129,193},{2,66},{66,130... | collective-permute-start | bytes 3080 | tf_op jit(solution)/shard_map/ppermute | solution.py:61
  47.4 12.6 %all-to-all-done.1 = f32[32,2,16,256]{3,1,2,0:T(2,128)S(1)} async-done(((f32[32,2,16,256]{3,1,2,0:T(2,128)}), f32[32,2,16,256]{3,1,2,0:T(2,128)S(1)}, u32[]{:S(2)}, u32[]{:S(2)}) %all-to-all-start.1) | async-done | bytes 1048608 | tf_op jit(solution)/shard_map/all_to_all | solution.py:34
  60.4 1.5 fusion.1
  61.9 1.3 collective-permute-start.1
  63.2 4.0 %collective-permute-start = (f32[2,1,256]{2,1,0:T(1,128)S(1)}, f32[2,1,256]{2,1,0:T(1,128)S(1)}, u32[]{:S(2)}, u32[]{:S(2)}) collective-permute-start(f32[2,1,256]{2,1,0:T(1,128)S(1)} %get-tuple-element.17), channel_id=1, source_target_pairs={{0,64},{64,128},{128,192},{1,65},{65,129},{129,193},{2,66},{66,130... | collective-permute-start | bytes 6152 | tf_op jit(solution)/shard_map/ppermute | solution.py:61
  67.1 1.8 %reduce-precision_convert_fusion = (bf16[272,256]{1,0:T(8,128)(2,1)S(1)}, bf16[272,256]{1,0:T(8,128)(2,1)S(1)}) fusion(s32[256]{0:T(256)} %copy-done.7, s32[272]{0:T(512)} %add_select_fusion.2, s32[256]{0:T(256)} %copy-done.6), kind=kLoop, calls=%fused_computation.24 | loop fusion | flops 1323008 | bytes 281664 | tf_op jit(solution)/shard_map/convert_element_type | solution.py:85
  69.0 1.5 collective-permute-start.7
  70.5 1.3 broadcast_in_dim.17
  71.8 6.4 %all-to-all-start.2 = ((f32[32,2,18,256]{3,1,2,0:T(2,128)}), f32[32,2,18,256]{3,1,2,0:T(2,128)}, u32[]{:S(2)}, u32[]{:S(2)}) async-start(f32[32,2,18,256]{3,1,2,0:T(2,128)} %broadcast_in_dim.17), calls=%async_computation.2 | async-start | bytes 2359296 | tf_op jit(solution)/shard_map/all_to_all | solution.py:39
  79.1 2.6 %collective-permute-start.9 = (f32[18,1,1]{1,2,0:T(1,128)S(1)}, f32[18,1,1]{1,2,0:T(1,128)S(1)}, u32[]{:S(2)}, u32[]{:S(2)}) collective-permute-start(f32[18,1,1]{1,2,0:T(1,128)S(1)} %get-tuple-element.20), channel_id=1, source_target_pairs={{1,0},{2,1},{3,2},{4,3},{5,4},{6,5},{7,6},{8,7},{9,8},{10,9},{11,1... | collective-permute-start | bytes 224 | tf_op jit(solution)/shard_map/ppermute | solution.py:64
  81.6 1.4 collective-permute-start.8
  83.1 3.2 %collective-permute-done.9 = f32[18,1,1]{1,2,0:T(1,128)S(1)} collective-permute-done((f32[18,1,1]{1,2,0:T(1,128)S(1)}, f32[18,1,1]{1,2,0:T(1,128)S(1)}, u32[]{:S(2)}, u32[]{:S(2)}) %collective-permute-start.9) | collective-permute-done | bytes 104 | tf_op jit(solution)/shard_map/ppermute | solution.py:64
  86.8 0.9 constant_dynamic-update-slice_fusion.2
  87.9 16.5 %collective-permute-start.5 = (f32[18,1,128]{2,1,0:T(1,128)S(1)}, f32[18,1,128]{2,1,0:T(1,128)S(1)}, u32[]{:S(2)}, u32[]{:S(2)}) collective-permute-start(f32[18,1,128]{2,1,0:T(1,128)S(1)} %get-tuple-element.6), channel_id=1, source_target_pairs={{1,0},{2,1},{3,2},{4,3},{5,4},{6,5},{7,6},{8,7},{9,8},{10,9},{11,1... | collective-permute-start | bytes 27656 | tf_op jit(solution)/shard_map/ppermute | solution.py:64
  105.3 5.0 %collective-permute-done.4 = f32[18,1,128]{2,1,0:T(1,128)S(1)} collective-permute-done((f32[18,1,128]{2,1,0:T(1,128)S(1)}, f32[18,1,128]{2,1,0:T(1,128)S(1)}, u32[]{:S(2)}, u32[]{:S(2)}) %collective-permute-start.4) | collective-permute-done | bytes 9248 | tf_op jit(solution)/shard_map/ppermute | solution.py:61
  110.5 1.9 %copy.44 = f32[32,2,18,256]{3,1,0,2:T(2,128)S(1)} copy(f32[32,2,18,256]{3,1,2,0:T(2,128)} %all-to-all-done.2) | data formatting | bytes 2359296 | tf_op jit(solution)/shard_map/all_to_all | solution.py:39
  112.4 1.4 broadcast_in_dim.18
  113.8 11.1 %all_to_all.21 = f32[2,32,2,18,256]{4,2,1,3,0:T(2,128)S(1)} all-to-all(f32[2,32,2,18,256]{4,2,1,3,0:T(2,128)S(1)} %broadcast_in_dim.18), channel_id=1, replica_groups=mesh['lat'=4,'lon_0'=8,'lon_1'=4,'lon_2'=2] {'lon_2'}, dimensions={0} | all-to-all | bytes 4718592 | tf_op jit(solution)/shard_map/all_to_all | solution.py:39
  124.9 2.3 %copy.45 = f32[32,2,2,18,256]{4,2,1,0,3:T(2,128)} copy(f32[32,2,2,18,256]{4,2,0,3,1:T(2,128)S(1)} %bitcast.51) | data formatting | bytes 4718592 | tf_op jit(solution)/shard_map/transpose | solution.py:51
  127.2 4.8 %reshape_reshape_reshape.7 = f32[128,18,2,128]{3,2,0,1:T(2,128)} reshape(f32[32,2,2,18,256]{4,2,1,0,3:T(2,128)} %copy.45) | data formatting | bytes 4718592 | tf_op jit(solution)/shard_map/reshape;reshape;reshape | solution.py:231
  131.9 3.1 %copy.46 = f32[128,2,18,128]{3,2,1,0:T(8,128)S(1)} copy(f32[128,2,18,128]{3,1,0,2:T(2,128)} %bitcast.54) | data formatting | bytes 4718592 | tf_op jit(solution)/shard_map/transpose | solution.py:231
  137.1 17.6 %tail.1 = f32[16,256,128]{2,1,0:T(8,128)} custom-call(f32[2,256,1152]{2,1,0:T(8,128)S(1)} %pad_maximum_fusion.mixed_hbm, f32[18,272,128]{2,1,0:T(8,128)S(1)} %select_maximum_fusion.field_hbm, f32[3,272,128]{2,1,0:T(8,128)S(1)} %pad_maximum_fusion.1.wet_ref, bf16[272,512]{1,0:T(8,128)(2,1)S(1)} %pad_maximum_fusion.2.table_ref, f32[128,128]{1,0:T(8,128)S(1)} %copy-done.1, ...), custom_call_target="tpu_custom_call" | custom-call | tf_op jit(solution)/shard_map/tail/pallas_call | solution.py:186
  (61 shorter events, 9.8 us)
Async XLA Ops:
  0.0 5.4 %copy-start.7 = (s32[256]{0:T(256)}, s32[256]{0:T(256)S(1)}, u32[]{:S(2)}) copy-start(s32[256]{0:T(256)S(1)} %get-tuple-element.25) | copy-start | bytes 3076
  0.9 4.5 %copy-start.6 = (s32[256]{0:T(256)}, s32[256]{0:T(256)S(1)}, u32[]{:S(2)}) copy-start(s32[256]{0:T(256)S(1)} %mul.69) | copy-start | bytes 3076
  22.8 10.9 %copy-start.4 = (f32[16,256,128]{2,1,0:T(8,128)S(1)}, f32[16,256,128]{2,1,0:T(8,128)}, u32[]{:S(2)}) copy-start(f32[16,256,128]{2,1,0:T(8,128)} %param.8) | copy-start | bytes 6291460
  22.8 23.3 %copy-start.5 = (f32[2,2,128,128]{3,2,1,0:T(8,128)S(1)}, f32[2,2,128,128]{3,2,1,0:T(8,128)}, u32[]{:S(2)}) copy-start(f32[2,2,128,128]{3,2,1,0:T(8,128)} %param.11) | copy-start | bytes 786436
  24.3 35.7 %all-to-all-start.1 = ((f32[32,2,16,256]{3,1,2,0:T(2,128)}), f32[32,2,16,256]{3,1,2,0:T(2,128)S(1)}, u32[]{:S(2)}, u32[]{:S(2)}) async-start(f32[32,2,16,256]{3,1,2,0:T(2,128)} %copy.38), calls=%async_computation.1 | async-start | bytes 2097152 | tf_op jit(solution)/shard_map/all_to_all | solution.py:34
  34.4 52.4 %collective-permute-start.2 = (f32[1,256,128]{2,1,0:T(8,128)}, f32[1,256,128]{2,1,0:T(8,128)}, u32[]{:S(2)}, u32[]{:S(2)}) collective-permute-start(f32[1,256,128]{2,1,0:T(8,128)} %get-tuple-element.12), channel_id=1, source_target_pairs={{0,64},{64,128},{128,192},{1,65},{65,129},{129,193},{2,66},{66,130... | collective-permute-start | bytes 393224 | tf_op jit(solution)/shard_map/ppermute | solution.py:61
  38.3 49.6 %collective-permute-start.3 = (f32[1,256,128]{2,1,0:T(8,128)}, f32[1,256,128]{2,1,0:T(8,128)S(1)}, u32[]{:S(2)}, u32[]{:S(2)}) collective-permute-start(f32[1,256,128]{2,1,0:T(8,128)} %get-tuple-element.11), channel_id=1, source_target_pairs={{64,0},{128,64},{192,128},{65,1},{129,65},{193,129},{66,2},{130,66... | collective-permute-start | bytes 393224 | tf_op jit(solution)/shard_map/ppermute | solution.py:64
  40.9 37.4 %collective-permute-start.6 = (f32[1,256,1]{1,2,0:T(1,128)}, f32[1,256,1]{1,2,0:T(1,128)}, u32[]{:S(2)}, u32[]{:S(2)}) collective-permute-start(f32[1,256,1]{1,2,0:T(1,128)} %get-tuple-element.22), channel_id=1, source_target_pairs={{0,64},{64,128},{128,192},{1,65},{65,129},{129,193},{2,66},{66,130... | collective-permute-start | bytes 3080 | tf_op jit(solution)/shard_map/ppermute | solution.py:61
  61.9 7.1 %collective-permute-start.1 = (f32[2,1,256]{2,1,0:T(1,128)S(1)}, f32[2,1,256]{2,1,0:T(1,128)S(1)}, u32[]{:S(2)}, u32[]{:S(2)}) collective-permute-start(f32[2,1,256]{2,1,0:T(1,128)S(1)} %get-tuple-element.18), channel_id=1, source_target_pairs={{64,0},{128,64},{192,128},{65,1},{129,65},{193,129},{66,2},{130,66... | collective-permute-start | bytes 6152 | tf_op jit(solution)/shard_map/ppermute | solution.py:64
  63.2 7.3 %collective-permute-start = (f32[2,1,256]{2,1,0:T(1,128)S(1)}, f32[2,1,256]{2,1,0:T(1,128)S(1)}, u32[]{:S(2)}, u32[]{:S(2)}) collective-permute-start(f32[2,1,256]{2,1,0:T(1,128)S(1)} %get-tuple-element.17), channel_id=1, source_target_pairs={{0,64},{64,128},{128,192},{1,65},{65,129},{129,193},{2,66},{66,130... | collective-permute-start | bytes 6152 | tf_op jit(solution)/shard_map/ppermute | solution.py:61
  69.0 10.0 %collective-permute-start.7 = (f32[1,256,1]{1,2,0:T(1,128)}, f32[1,256,1]{1,2,0:T(1,128)S(1)}, u32[]{:S(2)}, u32[]{:S(2)}) collective-permute-start(f32[1,256,1]{1,2,0:T(1,128)} %get-tuple-element.21), channel_id=1, source_target_pairs={{64,0},{128,64},{192,128},{65,1},{129,65},{193,129},{66,2},{130,66... | collective-permute-start | bytes 3080 | tf_op jit(solution)/shard_map/ppermute | solution.py:64
  71.8 38.6 %all-to-all-start.2 = ((f32[32,2,18,256]{3,1,2,0:T(2,128)}), f32[32,2,18,256]{3,1,2,0:T(2,128)}, u32[]{:S(2)}, u32[]{:S(2)}) async-start(f32[32,2,18,256]{3,1,2,0:T(2,128)} %broadcast_in_dim.17), calls=%async_computation.2 | async-start | bytes 2359296 | tf_op jit(solution)/shard_map/all_to_all | solution.py:39
  79.1 7.1 %collective-permute-start.9 = (f32[18,1,1]{1,2,0:T(1,128)S(1)}, f32[18,1,1]{1,2,0:T(1,128)S(1)}, u32[]{:S(2)}, u32[]{:S(2)}) collective-permute-start(f32[18,1,1]{1,2,0:T(1,128)S(1)} %get-tuple-element.20), channel_id=1, source_target_pairs={{1,0},{2,1},{3,2},{4,3},{5,4},{6,5},{7,6},{8,7},{9,8},{10,9},{11,1... | collective-permute-start | bytes 224 | tf_op jit(solution)/shard_map/ppermute | solution.py:64
  81.6 4.6 %collective-permute-start.8 = (f32[18,1,1]{1,2,0:T(1,128)S(1)}, f32[18,1,1]{1,2,0:T(1,128)S(1)}, u32[]{:S(2)}, u32[]{:S(2)}) collective-permute-start(f32[18,1,1]{1,2,0:T(1,128)S(1)} %get-tuple-element.19), channel_id=1, source_target_pairs={{0,1},{1,2},{2,3},{3,4},{4,5},{5,6},{6,7},{7,8},{8,9},{9,10},{10,1... | collective-permute-start | bytes 224 | tf_op jit(solution)/shard_map/ppermute | solution.py:61
  87.9 17.3 %collective-permute-start.5 = (f32[18,1,128]{2,1,0:T(1,128)S(1)}, f32[18,1,128]{2,1,0:T(1,128)S(1)}, u32[]{:S(2)}, u32[]{:S(2)}) collective-permute-start(f32[18,1,128]{2,1,0:T(1,128)S(1)} %get-tuple-element.6), channel_id=1, source_target_pairs={{1,0},{2,1},{3,2},{4,3},{5,4},{6,5},{7,6},{8,7},{9,8},{10,9},{11,1... | collective-permute-start | bytes 27656 | tf_op jit(solution)/shard_map/ppermute | solution.py:64
  104.4 5.8 %collective-permute-start.4 = (f32[18,1,128]{2,1,0:T(1,128)S(1)}, f32[18,1,128]{2,1,0:T(1,128)S(1)}, u32[]{:S(2)}, u32[]{:S(2)}) collective-permute-start(f32[18,1,128]{2,1,0:T(1,128)S(1)} %get-tuple-element.5), channel_id=1, source_target_pairs={{0,1},{1,2},{2,3},{3,4},{4,5},{5,6},{6,7},{7,8},{8,9},{9,10},{10,1... | collective-permute-start | bytes 27656 | tf_op jit(solution)/shard_map/ppermute | solution.py:61
  136.0 1.1 copy-start
  136.0 1.1 copy-start.1
  136.0 1.0 copy-start.2
  136.0 1.0 copy-start.3
where the time goes:
time: 156 us; the launch traced here: 155 us
  starting transfers between devices  52.7 us (34%)
  local copies, waits for them, and re-layouts  30.2 us (19%)
  waiting for transfers between devices  21.6 us (14%)
  blocking collectives  19.3 us (12%)
  Pallas kernels  17.6 us (11%)
  other arithmetic  6.88 us (4%)
  matrix products  5.93 us (4%)
    ppermute x5, starting transfers between devices, with_halo(): lax.ppermute(lax.slice_in_dim(block, 0, width, axis=dim), axis, backward)  23.1 us
    pallas_call x1, Pallas kernels, tail(): pl.pallas_call(functools.partial(tail_kernel, rows, width, scale, lat_axi...  17.6 us
    ppermute x5, starting transfers between devices, with_halo(): lax.ppermute(lax.slice_in_dim(block, block.shape[dim] - width, None, axis...  13.8 us
    all_to_all x1, waiting for transfers between devices, sum_by_axis(): return jnp.sum(lax.all_to_all(own, far, 0, 0, tiled=True), axis=0)  12.6 us
    all_to_all x1, blocking collectives, sent_to_all(): return lax.all_to_all(copies, axis, split_axis=0, concat_axis=0, tiled=True)  11.1 us
    all_to_all x1, starting transfers between devices, sum_by_axis(): return jnp.sum(lax.all_to_all(own, far, 0, 0, tiled=True), axis=0)  9.33 us
    all_to_all x1, blocking collectives, sent_and_summed(): blocks = lax.all_to_all(split_up(value, dim, size), axis, 0, 0, tiled=True)  8.24 us
    all_to_all x1, starting transfers between devices, sent_to_all(): return lax.all_to_all(copies, axis, split_axis=0, concat_axis=0, tiled=True)  6.41 us
  transfers between devices with their start and end apart: 12, of which 4 were waited for; matrix products, arithmetic and copies ran while one was open for 8% of the time, Pallas kernels for 0%

commit v1 on v0

--- a/solution.py
+++ b/solution.py
@@ -9,70 +9,12 @@
 from jax.sharding import Mesh
 from jax.sharding import PartitionSpec as P
 
-LON = ("lon_0", "lon_1", "lon_2")
+LON = ("z", "x", "core")
 HIGH = lax.Precision.HIGHEST
+MESH = pl.DeviceIdType.MESH
 PAD = 8
 BF = jnp.bfloat16
 F32 = jnp.float32
-
-
-def split_up(value, dim, size):
-    dims = value.shape
-    blocks = value.reshape(*dims[:dim], size, dims[dim] // size, *dims[dim + 1 :])
-    return jnp.moveaxis(blocks, dim, 0)
-
-
-def sent_and_summed(value, axis, dim):
-    size = lax.axis_size(axis)
-    blocks = lax.all_to_all(split_up(value, dim, size), axis, 0, 0, tiled=True)
-    return jnp.sum(blocks, axis=0)
-
-
-def sum_by_axis(value, axes, dim):
-    far, near = axes
-    own = sent_and_summed(split_up(value, dim, lax.axis_size(far)), near, dim + 1)
-    return jnp.sum(lax.all_to_all(own, far, 0, 0, tiled=True), axis=0)
-
-
-def sent_to_all(value, axis):
-    copies = jnp.broadcast_to(value, (lax.axis_size(axis), *value.shape))
-    return lax.all_to_all(copies, axis, split_axis=0, concat_axis=0, tiled=True)
-
-
-def joined_along(blocks, dim):
-    blocks = jnp.moveaxis(blocks, 0, dim)
-    dims = blocks.shape
-    return blocks.reshape(*dims[:dim], dims[dim] * dims[dim + 1], *dims[dim + 2 :])
-
-
-def whole_of(value, axes, dim):
-    far, near = axes
-    blocks = sent_to_all(sent_to_all(value, far), near)
-    return joined_along(blocks.swapaxes(0, 1).reshape(-1, *value.shape), dim)
-
-
-def with_halo(block, sides, width, periodic):
-    for axis, dim in sides:
-        count = lax.axis_size(axis)
-        forward = [(i, i + 1) for i in range(count - 1)]
-        if periodic:
-            forward.append((count - 1, 0))
-        backward = [(target, source) for source, target in forward]
-        low = lax.ppermute(
-            lax.slice_in_dim(block, block.shape[dim] - width, None, axis=dim), axis, forward
-        )
-        high = lax.ppermute(lax.slice_in_dim(block, 0, width, axis=dim), axis, backward)
-        block = jnp.concatenate([low, block, high], axis=dim)
-    return block
-
-
-def mix_modes(coeffs, weights):
-    w_real = weights[:, 0]
-    w_imag = weights[:, 1]
-    upper = jnp.concatenate([w_real, w_imag], -1)
-    lower = jnp.concatenate([-w_imag, w_real], -1)
-    blocks = jnp.concatenate([upper, lower], 1)
-    return jnp.einsum("mic,mcd->mid", coeffs, blocks, precision=HIGH)
 
 
 def halves(value):
@@ -209,50 +151,314 @@
     return jnp.cos(phase.astype(F32) * (2.0 * math.pi / total_lon))
 
 
+def exchange_kernel(
+    zs, xs, lats, scale,
+    field_hbm, wet, table, weight_hbm,
+    mixed_out, edged, wets,
+    field, weight, sent, got, sums, half_a, half_b, full_a, full_b, part, up, down, halo, whole,
+    load_sem, pair_sem, x_sem, z_sem, halo_sem, gz_sem, gx_sem, gp_sem, edge_sem, local_sem,
+):
+    rows, width, _ = field.shape
+    half = rows // 2
+    lanes = half * 128
+    cut = lanes // 2
+    lat, z, x, core = (lax.axis_index(name) for name in ("lat", "z", "x", "core"))
+    other = 1 - core
+
+    def wrap(value, size):
+        return lax.rem(value + size, size)
+
+    def device(lat=lat, z=z, x=x, core=core):
+        return {"lat": lat, "z": z, "x": x, "core": core}
+
+    def lon_at(step):
+        spot = wrap((z * xs + x) * 2 + core + step, zs * xs * 2)
+        return {"z": lax.div(spot, 2 * xs), "x": lax.rem(lax.div(spot, 2), xs), "core": lax.rem(spot, 2)}
+
+    right, left, across = wrap(x + 1, xs), wrap(x - 1, xs), wrap(x + 2, xs)
+    higher, lower = wrap(z + 1, zs), wrap(z - 1, zs)
+    south, north = wrap(lat + 1, lats), wrap(lat - 1, lats)
+    east, west = lon_at(1), lon_at(-1)
+
+    for i in range(rows):
+        pltpu.make_async_copy(field_hbm.at[i], field.at[i], load_sem.at[i]).start()
+    own_weight = pltpu.make_async_copy(weight_hbm, weight.at[core], local_sem.at[0])
+    own_weight.start()
+
+    barrier = pltpu.get_barrier_semaphore()
+    friends = [
+        device(core=other), device(x=right), device(x=left), device(z=higher), device(z=lower),
+        device(lat=south), device(lat=north), device(**east), device(**west),
+        device(lat=south, **east), device(lat=south, **west),
+        device(lat=north, **east), device(lat=north, **west),
+    ]
+    for friend in friends:
+        pl.semaphore_signal(barrier, inc=1, device_id=friend, device_id_type=MESH)
+
+    pending = []
+
+    def send(source, target, sems, index, where):
+        copy = pltpu.make_async_remote_copy(
+            src_ref=source, dst_ref=target, send_sem=sems.at[0, index], recv_sem=sems.at[1, index],
+            device_id=where, device_id_type=MESH,
+        )
+        copy.start()
+        pending.append(copy)
+        return copy
+
+    def coefficients(first):
+        pltpu.make_async_copy(field_hbm.at[0], field.at[0], load_sem.at[first]).wait()
+        pltpu.make_async_copy(field_hbm.at[0], field.at[0], load_sem.at[first + 1]).wait()
+        high, low = halves(jnp.concatenate([field[first], field[first + 1]], 1))
+        result = dot(table[...], jnp.concatenate([high, high], 0)) + dot(table[:, :width], low)
+        return result * scale
+
+    pairs = half // 2
+    pair_copies = []
+    for p in range(pairs):
+        sent[p] = coefficients(other * half + 2 * p)
+        if p == 0:
+            pl.semaphore_wait(barrier, len(friends))
+        pair_copies.append(send(sent.at[p], got.at[p], pair_sem, p, device(core=other)))
+    weight_copy = send(weight_hbm, weight.at[core], halo_sem, 1, device(core=other))
+
+    edges = []
+
+    def edge(source, target, where):
+        edges.append(send(source, target, edge_sem, len(edges), where))
+
+    edge(field_hbm.at[rows - 1], edged.at[0, pl.ds(PAD, width)], device(lat=south))
+    edge(field_hbm.at[0], edged.at[rows + 1, pl.ds(PAD, width)], device(lat=north))
+    edge(wet, wets.at[0, pl.ds(PAD, width)], device(lat=south))
+    edge(wet, wets.at[2, pl.ds(PAD, width)], device(lat=north))
+
+    for p in range(pairs):
+        mine = coefficients(core * half + 2 * p)
+        pair_copies[p].wait_recv()
+        mine = mine + got[p]
+        sums[:, :, :, pl.ds(p * 256, 256)] = mine.reshape(zs, xs, 8, 256)
+
+    order = (4, 3, 5, 2, 6, 1, 7, 0)
+    slices = [wrap(z + step, zs) for step in order]
+    low_lanes, high_lanes = pl.ds(0, cut), pl.ds(cut, cut)
+    firsts = []
+    for n, zz in enumerate(slices):
+        firsts.append((
+            send(sums.at[zz, across, :, low_lanes], half_a.at[n], x_sem, n, device(x=right)),
+            send(sums.at[zz, across, :, high_lanes], half_b.at[n], x_sem, 8 + n, device(x=left)),
+        ))
+    seconds = []
+    for n, zz in enumerate(slices):
+        firsts[n][0].wait_recv()
+        sums[zz, right, :, low_lanes] = sums[zz, right, :, low_lanes] + half_a[n]
+        to_right = send(sums.at[zz, right], full_a.at[n], x_sem, 16 + n, device(x=right))
+        firsts[n][1].wait_recv()
+        sums[zz, left, :, high_lanes] = sums[zz, left, :, high_lanes] + half_b[n]
+        to_left = send(sums.at[zz, left], full_b.at[n], x_sem, 24 + n, device(x=left))
+        seconds.append((to_right, to_left))
+
+    last = width - PAD
+    middle, ends = pl.ds(1, rows), (pl.ds(0, PAD), pl.ds(last, PAD))
+    outer = (pl.ds(PAD + width, PAD), pl.ds(0, PAD))
+
+    def send_edges():
+        for side, lon in ((0, west), (1, east)):
+            edge(field_hbm.at[:, ends[side]], edged.at[middle, outer[side]], device(**lon))
+            edge(wet.at[ends[side]], wets.at[1, outer[side]], device(**lon))
+            edge(field_hbm.at[rows - 1, ends[side]], edged.at[0, outer[side]], device(lat=south, **lon))
+            edge(wet.at[ends[side]], wets.at[0, outer[side]], device(lat=south, **lon))
+            edge(field_hbm.at[0, ends[side]], edged.at[rows + 1, outer[side]], device(lat=north, **lon))
+            edge(wet.at[ends[side]], wets.at[2, outer[side]], device(lat=north, **lon))
+
+    rising, falling = [], []
+    for n, zz in enumerate(slices):
+        seconds[n][0].wait_recv()
+        seconds[n][1].wait_recv()
+        total = sums[zz, x] + full_a[n] + full_b[n]
+        step = (n - 1) // 2
+        if n == 0:
+            part[n] = total
+            rising.append(send(part.at[n, :, low_lanes], up.at[0, :, low_lanes], z_sem, 0, device(z=higher)))
+            falling.append(send(part.at[n, :, high_lanes], down.at[0, :, high_lanes], z_sem, 4, device(z=lower)))
+            send_edges()
+        elif n == 7:
+            rising[3].wait_recv()
+            falling[3].wait_recv()
+            total = total + up[3] + down[3]
+        else:
+            rises = n % 2 == 1
+            chain, buffer = (rising, up) if rises else (falling, down)
+            chain[step].wait_recv()
+            if step == 0:
+                span = low_lanes if rises else high_lanes
+                part[n] = total
+                part[n, :, span] = part[n, :, span] + buffer[0, :, span]
+            else:
+                part[n] = total + buffer[step]
+            chain.append(send(
+                part.at[n], buffer.at[step + 1], z_sem, (0 if rises else 4) + step + 1,
+                device(z=higher if rises else lower),
+            ))
+
+    own_weight.wait()
+    weight_copy.wait_recv()
+    terms = jnp.concatenate([total[:, i * 128 : (i + 1) * 128] for i in range(half)], 0)
+    spot = lax.rem(lax.broadcasted_iota(jnp.int32, (half * 8, 128), 0), 8)
+    real, imag = jnp.zeros((half * 8, 128), F32), jnp.zeros((half * 8, 128), F32)
+    for m in range(4):
+        chosen = (spot == 2 * m) | (spot == 2 * m + 1)
+        picked = jnp.where(chosen, terms, 0.0)
+        real = real + jnp.dot(picked, weight[m // 2, m % 2, 0], precision=HIGH, preferred_element_type=F32)
+        imag = imag + jnp.dot(picked, weight[m // 2, m % 2, 1], precision=HIGH, preferred_element_type=F32)
+    even = lax.rem(spot, 2) == 0
+    mixed = real + jnp.where(even, -pltpu.roll(imag, half * 8 - 1, 0), pltpu.roll(imag, 1, 0))
+    for i in range(half):
+        whole[z, x, :, pl.ds(i * 128, 128)] = mixed[i * 8 : (i + 1) * 8]
+    halo[...] = jnp.where(core == 0, mixed[:8], mixed[(half - 1) * 8 :])
+    tail_lanes = pl.ds(lanes, 128)
+    row_copy = send(halo, whole.at[z, x, :, tail_lanes], halo_sem, 0, device(lat=wrap(lat - 1 + 2 * core, lats)))
+    row_copy.wait_recv()
+
+    front, back = pl.ds(0, cut), pl.ds(cut, lanes + 128 - cut)
+    order = (0, 7, 1, 6, 2, 5, 3, 4)
+    slices = [wrap(z + step, zs) for step in order]
+    rising, falling, sideways, relays, locals_, gathered = [], [], [], [], [], []
+
+    def spread(n):
+        zz = slices[n]
+        mine = whole.at[zz, x]
+        sideways.append((
+            send(mine, mine, gx_sem, n, device(x=right)),
+            send(mine, mine, gx_sem, 8 + n, device(x=left)),
+        ))
+
+    def relay(n):
+        zz = slices[n]
+        sideways[n][0].wait_recv()
+        from_left = whole.at[zz, left, :, front]
+        first = send(from_left, from_left, gx_sem, 16 + n, device(x=right))
+        sideways[n][1].wait_recv()
+        from_right = whole.at[zz, right, :, back]
+        second = send(from_right, from_right, gx_sem, 24 + n, device(x=left))
+        relays.append((first, second))
+
+    def finish(n):
+        zz = slices[n]
+        relays[n][0].wait_recv()
+        relays[n][1].wait_recv()
+        gathered.append(send(whole.at[zz], mixed_out.at[core, zz], gp_sem, n, device(core=other)))
+        kept = pltpu.make_async_copy(whole.at[zz], mixed_out.at[core, zz], local_sem.at[3 + n])
+        kept.start()
+        locals_.append(kept)
+
+    def climb(zz, step):
+        source = whole.at[zz, x] if step < 3 else whole.at[zz, x, :, front]
+        rising.append(send(source, source, gz_sem, step, device(z=higher)))
+
+    def descend(zz, step):
+        source = whole.at[zz, x] if step < 3 else whole.at[zz, x, :, back]
+        falling.append(send(source, source, gz_sem, 4 + step, device(z=lower)))
+
+    climb(slices[0], 0)
+    descend(slices[0], 0)
+    spread(0)
+    for n in range(1, 8):
+        step = (n - 1) // 2
+        if n == 7:
+            rising[3].wait_recv()
+            falling[3].wait_recv()
+        elif n % 2 == 1:
+            rising[step].wait_recv()
+            climb(slices[n], step + 1)
+        else:
+            falling[step].wait_recv()
+            descend(slices[n], step + 1)
+        spread(n)
+        relay(n - 1)
+        if n >= 2:
+            finish(n - 2)
+    relay(7)
+    finish(6)
+    finish(7)
+
+    inner = pltpu.make_async_copy(field, edged.at[middle, pl.ds(PAD, width)], local_sem.at[1])
+    inner.start()
+    inner_wet = pltpu.make_async_copy(wet, wets.at[1, pl.ds(PAD, width)], local_sem.at[2])
+    inner_wet.start()
+    for copy in edges + gathered:
+        copy.wait_recv()
+    for copy in pending:
+        copy.wait_send()
+    for copy in locals_ + [inner, inner_wet]:
+        copy.wait()
+
+
+def exchange(field, wet, table, weight, lats, zs, xs, scale):
+    rows, width, _ = field.shape
+    wide = width + 2 * PAD
+    lanes = rows // 2 * 128
+    vmem = pl.BlockSpec(memory_space=pltpu.VMEM)
+    hbm = pl.BlockSpec(memory_space=pl.ANY)
+    dma = pltpu.SemaphoreType.DMA
+    return pl.pallas_call(
+        functools.partial(exchange_kernel, zs, xs, lats, scale),
+        out_shape=(
+            jax.ShapeDtypeStruct((2, zs, xs, 8, lanes + 128), F32),
+            jax.ShapeDtypeStruct((rows + 2, wide, 128), F32),
+            jax.ShapeDtypeStruct((3, wide, 128), F32),
+        ),
+        in_specs=[hbm, vmem, vmem, hbm],
+        out_specs=(hbm, hbm, hbm),
+        scratch_shapes=[
+            pltpu.VMEM((rows, width, 128), F32),
+            pltpu.VMEM((2, *weight.shape), F32),
+            pltpu.VMEM((rows // 4, 256, 256), F32),
+            pltpu.VMEM((rows // 4, 256, 256), F32),
+            pltpu.VMEM((zs, xs, 8, lanes), F32),
+            pltpu.VMEM((zs, 8, lanes // 2), F32),
+            pltpu.VMEM((zs, 8, lanes // 2), F32),
+            pltpu.VMEM((zs, 8, lanes), F32),
+            pltpu.VMEM((zs, 8, lanes), F32),
+            pltpu.VMEM((zs, 8, lanes), F32),
+            pltpu.VMEM((4, 8, lanes), F32),
+            pltpu.VMEM((4, 8, lanes), F32),
+            pltpu.VMEM((8, 128), F32),
+            pltpu.VMEM((zs, xs, 8, lanes + 128), F32),
+            dma((rows,)), dma((2, 4)), dma((2, 32)), dma((2, 8)), dma((2, 2)), dma((2, 8)),
+            dma((2, 32)), dma((2, 8)), dma((2, 16)), dma((11,)),
+        ],
+        compiler_params=pltpu.CompilerParams(
+            collective_id=0, has_side_effects=True, vmem_limit_bytes=32 << 20
+        ),
+        name="exchange",
+    )(field, wet, table, weight)
+
+
 def per_device(field, ocean, modes, spectral_weight, local_weight, layer_bias, conv_weight, conv_bias):
     rows, width, channels = field.shape
-    lon_count = lax.axis_size(LON)
-    total_lon = width * lon_count
+    lats, zs, xs = (lax.axis_size(name) for name in ("lat", "z", "x"))
+    total_lon = width * zs * xs * 2
     total_modes = modes.shape[0]
     lon_start = lax.axis_index(LON) * width
-    scale = 2.0 / math.sqrt(total_modes)
     pair = jnp.repeat(modes, 2)
     parity = jnp.arange(2 * total_modes, dtype=jnp.int32) % 2
+    own_ids = lon_start + jnp.arange(width, dtype=jnp.int32)
+    forward = jnp.concatenate(stored_halves(table_of(own_ids[None], pair[:, None], parity[:, None], total_lon)), 1)
+    wet = jnp.pad(ocean.astype(F32).T, ((0, 0), (1, 127 - rows)))
+    mixed, edged, wets = exchange(
+        field, wet, forward, spectral_weight, lats, zs, xs, 1.0 / math.sqrt(total_lon)
+    )
     lon_ids = (lon_start - PAD + jnp.arange(width + 2 * PAD, dtype=jnp.int32) + total_lon) % total_lon
     inverse = jnp.concatenate(stored_halves(table_of(lon_ids[:, None], pair[None], parity[None], total_lon)), 1)
-    own_ids = lon_start + jnp.arange(width, dtype=jnp.int32)
-    forward = table_of(own_ids[None], pair[:, None], parity[:, None], total_lon)
-    partial = jnp.einsum("kj,ijc->kic", forward, field, precision=HIGH) / math.sqrt(total_lon)
-    partial = partial.reshape(total_modes, 2, rows, channels).swapaxes(1, 2).reshape(total_modes, rows, 2 * channels)
-    own_coeffs = sum_by_axis(partial, (("lon_0", "lon_1"), "lon_2"), 0)
-    own_mixed = mix_modes(own_coeffs, spectral_weight)
-    own_mixed = with_halo(own_mixed, (("lat", 1),), 1, False)
-    mixed = whole_of(own_mixed, (("lon_0", "lon_1"), "lon_2"), 0)
-    mixed = mixed.reshape(total_modes, rows + 2, 2, channels).swapaxes(1, 2)
-    mixed = mixed.reshape(2 * total_modes, (rows + 2) * channels)
-    half = rows // 2 * channels
-    last = rows * channels + channels
-    parts = jnp.stack([
-        jnp.concatenate([mixed[:, channels : channels + half], mixed[:, last:]], 1),
-        jnp.concatenate([mixed[:, channels + half : last], mixed[:, :channels]], 1),
-    ])
-    gap = ((0, 0), (PAD - 1, PAD - 1), (0, 0))
-    edged = with_halo(field, (("lat", 0),), 1, False)
-    edged = jnp.pad(with_halo(edged, ((LON, 1),), 1, True), gap)
-    wet = with_halo(ocean.astype(F32)[:, :, None], (("lat", 0),), 1, False)
-    wet = with_halo(wet, ((LON, 1),), 1, True)
-    wet = jnp.pad(wet, gap)[:, :, 0].T
-    mid = jnp.pad(wet, ((0, 0), (0, 128 - rows - 2)))
-    above = jnp.pad(wet[:, :1], ((0, 0), (rows, 127 - rows)))
-    below = jnp.pad(wet[:, rows + 1 :], ((0, 0), (1, 126)))
+    mixed = mixed.reshape(2, 2 * total_modes, -1)
     return tail(
-        parts, edged, jnp.stack([above, mid, below]), inverse, local_weight, layer_bias,
-        conv_weight, conv_bias, rows, width, scale, "lat", lax.axis_size("lat"),
+        mixed, edged, wets, inverse, local_weight, layer_bias,
+        conv_weight, conv_bias, rows, width, 2.0 / math.sqrt(total_modes), "lat", lats,
     )
 
 
 def solution(mesh):
-    split = Mesh(mesh.devices.reshape(mesh.shape["lat"], 8, 4, 2), ("lat", "lon_0", "lon_1", "lon_2"))
+    split = Mesh(mesh.devices.reshape(mesh.shape["lat"], 8, 4, 2), ("lat", *LON))
     placed = (P("lat", LON, None), P("lat", LON), P(), P(LON, None, None, None), P(), P(), P(), P())
     return jax.shard_map(
         per_device, mesh=split, in_specs=placed, out_specs=P("lat", LON, None), check_vma=False

time: 156 us -> 87.7 us (0.56)
  Pallas kernels: 17.6 us -> 82 us
  starting transfers between devices: 52.7 us -> 0 us
  local copies, waits for them, and re-layouts: 30.2 us -> 2.03 us
  waiting for transfers between devices: 21.6 us -> 0 us
  blocking collectives: 19.3 us -> 0 us
  matrix products: 5.93 us -> 0 us
  other arithmetic: 6.88 us -> 3.15 us
    pallas_call x0 -> x1, Pallas kernels: none -> 64.4 us  [exchange(): pl.pallas_call(functools.partial(exchange_kernel, zs, xs, lats, scale), o...]
    ppermute x10 -> x0, starting transfers between devices: 36.9 us -> none  [the longest x5 23.1 us: with_halo(): lax.ppermute(lax.slice_in_dim(block, 0, width, axis=dim), axis, backward)]
    all_to_all x2 -> x0, blocking collectives: 19.3 us -> none  [the longest x1 11.1 us: sent_to_all(): return lax.all_to_all(copies, axis, split_axis=0, concat_axis=0, tiled=True)]
    all_to_all x2 -> x0, starting transfers between devices: 15.7 us -> none  [the longest x1 9.33 us: sum_by_axis(): return jnp.sum(lax.all_to_all(own, far, 0, 0, tiled=True), axis=0)]
    all_to_all x2 -> x0, waiting for transfers between devices: 12.6 us -> none  [the longest x1 12.6 us: sum_by_axis(): return jnp.sum(lax.all_to_all(own, far, 0, 0, tiled=True), axis=0)]
    ppermute x10 -> x0, waiting for transfers between devices: 8.96 us -> none  [the longest x5 5 us: with_halo(): lax.ppermute(lax.slice_in_dim(block, block.shape[dim] - width, None, axis...]
    transpose x4 -> x0, local copies, waits for them, and re-layouts: 8.61 us -> none  [the longest x1 3.21 us: split_up(): return jnp.moveaxis(blocks, dim, 0)]
    another operation x4 -> x0, local copies, waits for them, and re-layouts: 7.58 us -> none  [the longest x1 4.75 us: per_device(): mixed = mixed.reshape(total_modes, rows + 2, 2, channels).swapaxes(1, 2)]
  transfers between devices with their start and end apart: 12 -> 0, of which waited for: 4 -> 0; matrix products, arithmetic and copies ran while one was open for 8% -> 0% of each run, Pallas kernels for 0% -> 0%
where the time goes in v1:
time: 87.7 us; the launch traced here: 87.3 us
  Pallas kernels  82 us (94%)
  other arithmetic  3.15 us (4%)
  local copies, waits for them, and re-layouts  2.03 us (2%)
    pallas_call x1, Pallas kernels, exchange(): pl.pallas_call(functools.partial(exchange_kernel, zs, xs, lats, scale), o...  64.4 us
    pallas_call x1, Pallas kernels, tail(): pl.pallas_call(functools.partial(tail_kernel, rows, width, scale, lat_axi...  17.6 us
    convert_element_type x2, other arithmetic, stored_halves(): return (high.astype(BF), (value - high).astype(BF))  2.23 us

profile of v1, /device:TPU:1, one launch (start us, length us, event | category | flops | bytes accessed | tf_op | source)
XLA Modules:
  0.0 87.3 jit_solution(16391092610099493915)
XLA Ops:
  0.0 0.0 copy-start
  0.0 0.9 convert_element_type.23
  0.9 0.7 broadcast_in_dim.2
  1.6 0.1 mul.69
  1.8 0.1 copy.10
  1.9 0.0 copy-start.1
  1.9 0.1 pad.4.wet
  2.0 1.1 %reduce-precision_convert_fusion.1 = (bf16[256,256]{1,0:T(8,128)(2,1)S(1)}, bf16[256,256]{1,0:T(8,128)(2,1)S(1)}) fusion(s32[256]{0:T(256)S(1)} %get-tuple-element.15, s32[256]{0:T(256)S(1)} %get-tuple-element.16, s32[256]{0:T(256)S(1)} %mul.69), kind=kLoop, calls=%fused_computation.9 | loop fusion | flops 1245184 | bytes 265216 | tf_op jit(solution)/shard_map/convert_element_type | solution.py:27
  3.1 1.1 %reduce-precision_convert_fusion = (bf16[272,256]{1,0:T(8,128)(2,1)S(1)}, bf16[272,256]{1,0:T(8,128)(2,1)S(1)}) fusion(s32[256]{0:T(256)S(1)} %get-tuple-element.15, s32[272]{0:T(512)S(1)} %add_select_fusion.2, s32[256]{0:T(256)S(1)} %mul.69), kind=kLoop, calls=%fused_computation.4 | loop fusion | flops 1323008 | bytes 281664 | tf_op jit(solution)/shard_map/convert_element_type | solution.py:27
  4.3 0.0 copy-done
  4.3 0.0 copy-start.2
  4.3 0.9 %copy-done.2 = f32[2,2,128,128]{3,2,1,0:T(8,128)S(1)} copy-done((f32[2,2,128,128]{3,2,1,0:T(8,128)S(1)}, f32[2,2,128,128]{3,2,1,0:T(8,128)}, u32[]{:S(2)}) %copy-start.2) | copy-done | bytes 262168
  5.2 0.0 copy-start.3
  5.2 0.0 copy-start.4
  5.2 0.0 copy-start.5
  5.2 64.4 %exchange.1 = (f32[2,8,4,8,1152]{4,3,2,1,0:T(8,128)S(1)}, f32[18,272,128]{2,1,0:T(8,128)S(1)}, f32[3,272,128]{2,1,0:T(8,128)S(1)}) custom-call(f32[16,256,128]{2,1,0:T(8,128)S(1)} %copy-done, f32[256,128]{1,0:T(8,128)S(1)} %pad.4.wet, bf16[256,512]{1,0:T(8,128)(2,1)S(1)} %pad_maximum_fusion.1.table, f32[2,2,128,128]{3,2,1,0:T(8,128)S(1)} %copy-done.2), custom_call_target="tpu_custom_call" | custom-call | tf_op jit(solution)/shard_map/exchange/pallas_call | solution.py:403
  69.6 0.0 copy-done.1
  69.6 0.0 copy-done.3
  69.7 0.0 copy-done.4
  69.7 0.0 copy-done.5
  69.7 17.6 %tail.1 = f32[16,256,128]{2,1,0:T(8,128)} custom-call(f32[2,256,1152]{2,1,0:T(8,128)S(1)} %bitcast.4, f32[18,272,128]{2,1,0:T(8,128)S(1)} %get-tuple-element.9.field_hbm, f32[3,272,128]{2,1,0:T(8,128)S(1)} %get-tuple-element.10.wet_ref, bf16[272,512]{1,0:T(8,128)(2,1)S(1)} %pad_maximum_fusion.table_ref, f32[128,128]{1,0:T(8,128)S(1)} %copy-done.3, ...), custom_call_target="tpu_custom_call" | custom-call | tf_op jit(solution)/shard_map/tail/pallas_call | solution.py:128
  (4 shorter events, 0.1 us)
Async XLA Ops:
  0.0 4.3 %copy-start = (f32[16,256,128]{2,1,0:T(8,128)S(1)}, f32[16,256,128]{2,1,0:T(8,128)}, u32[]{:S(2)}) copy-start(f32[16,256,128]{2,1,0:T(8,128)} %field_hbm.1) | copy-start | bytes 6291460
  1.9 67.8 %copy-start.1 = (f32[3,3,128,128]{3,2,1,0:T(8,128)S(1)}, f32[3,3,128,128]{3,2,1,0:T(8,128)}, u32[]{:S(2)}) copy-start(f32[3,3,128,128]{3,2,1,0:T(8,128)} %conv_ref.1) | copy-start | bytes 1769476
  4.3 1.0 %copy-start.2 = (f32[2,2,128,128]{3,2,1,0:T(8,128)S(1)}, f32[2,2,128,128]{3,2,1,0:T(8,128)}, u32[]{:S(2)}) copy-start(f32[2,2,128,128]{3,2,1,0:T(8,128)} %weight_hbm.1) | copy-start | bytes 786436
  5.2 64.4 %copy-start.3 = (f32[128,128]{1,0:T(8,128)S(1)}, f32[128,128]{1,0:T(8,128)}, u32[]{:S(2)}) copy-start(f32[128,128]{1,0:T(8,128)} %local_ref.1) | copy-start | bytes 196612
  5.2 64.4 %copy-start.4 = (f32[128]{0:T(128)S(1)}, f32[128]{0:T(128)}, u32[]{:S(2)}) copy-start(f32[128]{0:T(128)} %param.13) | copy-start | bytes 1540
  5.2 64.4 %copy-start.5 = (f32[128]{0:T(128)S(1)}, f32[128]{0:T(128)}, u32[]{:S(2)}) copy-start(f32[128]{0:T(128)} %param.15) | copy-start | bytes 1540

commit v2 on v1

--- a/solution.py
+++ b/solution.py
@@ -22,11 +22,6 @@
     return high, (value - high.astype(F32)).astype(BF)
 
 
-def stored_halves(value):
-    high = lax.reduce_precision(value, 8, 7)
-    return high.astype(BF), (value - high).astype(BF)
-
-
 def dot(a, b):
     return jnp.dot(a, b, preferred_element_type=F32)
 
@@ -37,25 +32,13 @@
 
 def tail_kernel(
     rows, width, scale, lat_axis, lat_count,
-    mixed_hbm, field_hbm, wet_ref, table_ref, local_ref, bias_ref, conv_ref, conv_bias_ref,
+    mixed, field, wet_ref, table_ref, local_ref, bias_ref, conv_ref, conv_bias_ref,
     out_hbm,
-    mixed, field, hidden, mask, taps, local, out, sem_in, sem_out,
+    hidden, mask, taps, local, out, sem_out,
 ):
     ext = rows + 2
     wide = width + 2 * PAD
     half = rows // 2
-
-    def mixed_copy(r):
-        part, block = (1, half) if r == 0 else (0, half) if r == ext - 1 else divmod(r - 1, half)
-        source = mixed_hbm.at[part, :, pl.ds(block * 128, 128)]
-        return pltpu.make_async_copy(source, mixed.at[r], sem_in.at[0, r])
-
-    def field_copy(r):
-        return pltpu.make_async_copy(field_hbm.at[r], field.at[r], sem_in.at[1, r])
-
-    for r in range(ext):
-        mixed_copy(r).start()
-        field_copy(r).start()
 
     high, low = halves(local_ref[...])
     both = jnp.concatenate([high, low], 1)
@@ -78,11 +61,11 @@
 
     @pl.loop(0, ext)
     def _(r):
-        pltpu.make_async_copy(field_hbm.at[0], field.at[0], sem_in.at[1, r]).wait()
-        pltpu.make_async_copy(
-            mixed_hbm.at[0, :, pl.ds(0, 128)], mixed.at[0], sem_in.at[0, r]
-        ).wait()
-        high, low = halves(mixed[r])
+        outer = (r == 0) | (r == ext - 1)
+        second = (r > half) & (r < ext - 1) | (r == 0)
+        block = jnp.where(outer, half, lax.rem(r + half - 1, half))
+        spot = pl.ds(pl.multiple_of(block * 128, 128), 128)
+        high, low = halves(mixed[jnp.where(second, 1, 0), :, spot])
         both = jnp.concatenate([high, low], 1)
         spectral = lane_sum(dot(table_ref[...], jnp.concatenate([both, both], 0))) * scale
         high, low = halves(field[r])
@@ -128,17 +111,14 @@
     return pl.pallas_call(
         functools.partial(tail_kernel, rows, width, scale, lat_axis, lat_count),
         out_shape=jax.ShapeDtypeStruct((rows, width, 128), F32),
-        in_specs=[hbm, hbm] + [vmem] * 6,
+        in_specs=[vmem] * 8,
         out_specs=hbm,
         scratch_shapes=[
-            pltpu.VMEM((ext, 256, 128), F32),
-            pltpu.VMEM((ext, wide, 128), F32),
             pltpu.VMEM((rows + 4, wide, 768), BF),
             pltpu.VMEM((ext, wide, 128), F32),
             pltpu.VMEM((768, 768), BF),
             pltpu.VMEM((256, 256), BF),
             pltpu.VMEM((rows, width, 128), F32),
-            pltpu.SemaphoreType.DMA((2, ext)),
             pltpu.SemaphoreType.DMA((rows // 2,)),
         ],
         compiler_params=pltpu.CompilerParams(vmem_limit_bytes=40 << 20),
@@ -146,22 +126,19 @@
     )(mixed, field, wet, table, local_weight, layer_bias.reshape(1, 128), conv_weight, conv_bias.reshape(1, 128))
 
 
-def table_of(lon_ids, modes_of, parity, total_lon):
-    phase = (modes_of * lon_ids + parity * (total_lon // 4)) % total_lon
-    return jnp.cos(phase.astype(F32) * (2.0 * math.pi / total_lon))
-
-
 def exchange_kernel(
     zs, xs, lats, scale,
-    field_hbm, wet, table, weight_hbm,
-    mixed_out, edged, wets,
-    field, weight, sent, got, sums, half_a, half_b, full_a, full_b, part, up, down, halo, whole,
+    field_hbm, ocean_hbm, modes_hbm, weight_hbm,
+    mixed_out, edged, wets, table_out,
+    ocean, modes, wet, table, turned, field, weight, sent, got, sums, half_a, half_b, full_a, full_b, part, up, down, halo, whole,
     load_sem, pair_sem, x_sem, z_sem, halo_sem, gz_sem, gx_sem, gp_sem, edge_sem, local_sem,
 ):
     rows, width, _ = field.shape
     half = rows // 2
     lanes = half * 128
     cut = lanes // 2
+    wide = width + 2 * PAD
+    total_lon = zs * xs * 2 * width
     lat, z, x, core = (lax.axis_index(name) for name in ("lat", "z", "x", "core"))
     other = 1 - core
 
@@ -180,20 +157,50 @@
     south, north = wrap(lat + 1, lats), wrap(lat - 1, lats)
     east, west = lon_at(1), lon_at(-1)
 
+    small = [
+        pltpu.make_async_copy(modes_hbm, modes, local_sem.at[12]),
+        pltpu.make_async_copy(ocean_hbm, ocean, local_sem.at[13]),
+    ]
+    for copy in small:
+        copy.start()
     for i in range(rows):
-        pltpu.make_async_copy(field_hbm.at[i], field.at[i], load_sem.at[i]).start()
+        row = (other if i < half else core) * half + i % half
+        pltpu.make_async_copy(field_hbm.at[row], field.at[row], load_sem.at[row]).start()
     own_weight = pltpu.make_async_copy(weight_hbm, weight.at[core], local_sem.at[0])
     own_weight.start()
 
     barrier = pltpu.get_barrier_semaphore()
+    beyond, behind = wrap(z + 2, zs), wrap(z - 2, zs)
     friends = [
         device(core=other), device(x=right), device(x=left), device(z=higher), device(z=lower),
-        device(lat=south), device(lat=north), device(**east), device(**west),
-        device(lat=south, **east), device(lat=south, **west),
-        device(lat=north, **east), device(lat=north, **west),
+        device(z=beyond), device(z=behind), device(lat=south), device(lat=north),
+        device(**east), device(**west),
     ]
     for friend in friends:
         pl.semaphore_signal(barrier, inc=1, device_id=friend, device_id_type=MESH)
+
+    for copy in small:
+        copy.wait()
+    count = 2 * modes.shape[1]
+    slot = lax.broadcasted_iota(jnp.int32, (count // 2, count), 1)
+    spread_out = lax.div(slot, 2) == lax.broadcasted_iota(jnp.int32, (count // 2, count), 0)
+    pair = jnp.dot(
+        jnp.broadcast_to(modes[...].astype(F32), (8, count // 2)), spread_out.astype(F32),
+        precision=HIGH, preferred_element_type=F32,
+    )[:1].astype(jnp.int32)
+    start = ((z * xs + x) * 2 + core) * width - PAD + total_lon
+    lon = start + lax.broadcasted_iota(jnp.int32, (wide, count), 0)
+    odd = lax.broadcasted_iota(jnp.int32, (wide, count), 1) & 1
+    phase = (pair * (lon & (total_lon - 1)) + odd * (total_lon // 4)) & (total_lon - 1)
+    wave = jnp.cos(phase.astype(F32) * (2.0 * math.pi / total_lon))
+    high, low = halves(wave)
+    turned[:, :count] = high
+    turned[:, count:] = low
+    high, low = halves(wave[PAD : PAD + width].T)
+    table[:, :width] = high
+    table[:, width:] = low
+    dry = jnp.zeros((128 - rows, width), F32)
+    wet[...] = pltpu.roll(jnp.concatenate([ocean[...].astype(F32), dry], 0).T, 1, 1)
 
     pending = []
 
@@ -237,6 +244,15 @@
         pair_copies[p].wait_recv()
         mine = mine + got[p]
         sums[:, :, :, pl.ds(p * 256, 256)] = mine.reshape(zs, xs, 8, 256)
+
+    middle = pl.ds(PAD, width)
+    inner = [
+        pltpu.make_async_copy(field, edged.at[pl.ds(1, rows), middle], local_sem.at[1]),
+        pltpu.make_async_copy(wet, wets.at[1, middle], local_sem.at[2]),
+    ]
+    kept_table = pltpu.make_async_copy(turned, table_out, local_sem.at[11])
+    for copy in inner + [kept_table]:
+        copy.start()
 
     order = (4, 3, 5, 2, 6, 1, 7, 0)
     slices = [wrap(z + step, zs) for step in order]
@@ -257,18 +273,14 @@
         to_left = send(sums.at[zz, left], full_b.at[n], x_sem, 24 + n, device(x=left))
         seconds.append((to_right, to_left))
 
-    last = width - PAD
-    middle, ends = pl.ds(1, rows), (pl.ds(0, PAD), pl.ds(last, PAD))
-    outer = (pl.ds(PAD + width, PAD), pl.ds(0, PAD))
-
     def send_edges():
-        for side, lon in ((0, west), (1, east)):
-            edge(field_hbm.at[:, ends[side]], edged.at[middle, outer[side]], device(**lon))
-            edge(wet.at[ends[side]], wets.at[1, outer[side]], device(**lon))
-            edge(field_hbm.at[rows - 1, ends[side]], edged.at[0, outer[side]], device(lat=south, **lon))
-            edge(wet.at[ends[side]], wets.at[0, outer[side]], device(lat=south, **lon))
-            edge(field_hbm.at[0, ends[side]], edged.at[rows + 1, outer[side]], device(lat=north, **lon))
-            edge(wet.at[ends[side]], wets.at[2, outer[side]], device(lat=north, **lon))
+        for copy in edges:
+            copy.wait_recv()
+        for copy in inner:
+            copy.wait()
+        for source, target, lon in ((PAD, PAD + width, west), (width, 0, east)):
+            edge(edged.at[:, pl.ds(source, PAD)], edged.at[:, pl.ds(target, PAD)], device(**lon))
+            edge(wets.at[:, pl.ds(source, PAD)], wets.at[:, pl.ds(target, PAD)], device(**lon))
 
     rising, falling = [], []
     for n, zz in enumerate(slices):
@@ -322,7 +334,7 @@
     front, back = pl.ds(0, cut), pl.ds(cut, lanes + 128 - cut)
     order = (0, 7, 1, 6, 2, 5, 3, 4)
     slices = [wrap(z + step, zs) for step in order]
-    rising, falling, sideways, relays, locals_, gathered = [], [], [], [], [], []
+    sideways, relays, locals_, gathered = [], [], [], []
 
     def spread(n):
         zz = slices[n]
@@ -351,53 +363,51 @@
         kept.start()
         locals_.append(kept)
 
-    def climb(zz, step):
-        source = whole.at[zz, x] if step < 3 else whole.at[zz, x, :, front]
-        rising.append(send(source, source, gz_sem, step, device(z=higher)))
-
-    def descend(zz, step):
-        source = whole.at[zz, x] if step < 3 else whole.at[zz, x, :, back]
-        falling.append(send(source, source, gz_sem, 4 + step, device(z=lower)))
-
-    climb(slices[0], 0)
-    descend(slices[0], 0)
+    def along(n, where, index, span=None):
+        source = whole.at[slices[n], x] if span is None else whole.at[slices[n], x, :, span]
+        return send(source, source, gz_sem, index, device(z=where))
+
+    far_up, far_down = along(0, beyond, 2), along(0, behind, 3)
+    near_up, near_down = along(0, higher, 0), along(0, lower, 1)
     spread(0)
-    for n in range(1, 8):
-        step = (n - 1) // 2
-        if n == 7:
-            rising[3].wait_recv()
-            falling[3].wait_recv()
-        elif n % 2 == 1:
-            rising[step].wait_recv()
-            climb(slices[n], step + 1)
-        else:
-            falling[step].wait_recv()
-            descend(slices[n], step + 1)
-        spread(n)
-        relay(n - 1)
-        if n >= 2:
-            finish(n - 2)
-    relay(7)
+    near_up.wait_recv()
+    spread(1)
+    near_down.wait_recv()
+    spread(2)
+    far_up.wait_recv()
+    next_up, half_up = along(3, higher, 4), along(3, beyond, 6, front)
+    far_down.wait_recv()
+    next_down, half_down = along(4, lower, 5), along(4, behind, 7, back)
+    spread(3)
+    spread(4)
+    for n in range(3):
+        relay(n)
+    next_up.wait_recv()
+    spread(5)
+    next_down.wait_recv()
+    spread(6)
+    half_up.wait_recv()
+    half_down.wait_recv()
+    spread(7)
+    finish(0)
+    for n in range(3, 8):
+        relay(n)
+        finish(n - 2)
     finish(6)
     finish(7)
 
-    inner = pltpu.make_async_copy(field, edged.at[middle, pl.ds(PAD, width)], local_sem.at[1])
-    inner.start()
-    inner_wet = pltpu.make_async_copy(wet, wets.at[1, pl.ds(PAD, width)], local_sem.at[2])
-    inner_wet.start()
-    for copy in edges + gathered:
+    for copy in edges[4:] + gathered:
         copy.wait_recv()
     for copy in pending:
         copy.wait_send()
-    for copy in locals_ + [inner, inner_wet]:
+    for copy in locals_ + [kept_table]:
         copy.wait()
 
 
-def exchange(field, wet, table, weight, lats, zs, xs, scale):
+def exchange(field, ocean, modes, weight, lats, zs, xs, scale):
     rows, width, _ = field.shape
     wide = width + 2 * PAD
     lanes = rows // 2 * 128
-    vmem = pl.BlockSpec(memory_space=pltpu.VMEM)
     hbm = pl.BlockSpec(memory_space=pl.ANY)
     dma = pltpu.SemaphoreType.DMA
     return pl.pallas_call(
@@ -406,10 +416,16 @@
             jax.ShapeDtypeStruct((2, zs, xs, 8, lanes + 128), F32),
             jax.ShapeDtypeStruct((rows + 2, wide, 128), F32),
             jax.ShapeDtypeStruct((3, wide, 128), F32),
+            jax.ShapeDtypeStruct((wide, 512), BF),
         ),
-        in_specs=[hbm, vmem, vmem, hbm],
-        out_specs=(hbm, hbm, hbm),
+        in_specs=[hbm] * 4,
+        out_specs=(hbm, hbm, hbm, hbm),
         scratch_shapes=[
+            pltpu.VMEM(ocean.shape, jnp.int32),
+            pltpu.VMEM((1, modes.size), jnp.int32),
+            pltpu.VMEM((width, 128), F32),
+            pltpu.VMEM((256, 2 * width), BF),
+            pltpu.VMEM((wide, 512), BF),
             pltpu.VMEM((rows, width, 128), F32),
             pltpu.VMEM((2, *weight.shape), F32),
             pltpu.VMEM((rows // 4, 256, 256), F32),
@@ -425,13 +441,13 @@
             pltpu.VMEM((8, 128), F32),
             pltpu.VMEM((zs, xs, 8, lanes + 128), F32),
             dma((rows,)), dma((2, 4)), dma((2, 32)), dma((2, 8)), dma((2, 2)), dma((2, 8)),
-            dma((2, 32)), dma((2, 8)), dma((2, 16)), dma((11,)),
+            dma((2, 32)), dma((2, 8)), dma((2, 8)), dma((14,)),
         ],
         compiler_params=pltpu.CompilerParams(
             collective_id=0, has_side_effects=True, vmem_limit_bytes=32 << 20
         ),
         name="exchange",
-    )(field, wet, table, weight)
+    )(*(pltpu.with_memory_space_constraint(a, pltpu.HBM) for a in (field, ocean, modes.reshape(1, -1), weight)))
 
 
 def per_device(field, ocean, modes, spectral_weight, local_weight, layer_bias, conv_weight, conv_bias):
@@ -439,17 +455,9 @@
     lats, zs, xs = (lax.axis_size(name) for name in ("lat", "z", "x"))
     total_lon = width * zs * xs * 2
     total_modes = modes.shape[0]
-    lon_start = lax.axis_index(LON) * width
-    pair = jnp.repeat(modes, 2)
-    parity = jnp.arange(2 * total_modes, dtype=jnp.int32) % 2
-    own_ids = lon_start + jnp.arange(width, dtype=jnp.int32)
-    forward = jnp.concatenate(stored_halves(table_of(own_ids[None], pair[:, None], parity[:, None], total_lon)), 1)
-    wet = jnp.pad(ocean.astype(F32).T, ((0, 0), (1, 127 - rows)))
-    mixed, edged, wets = exchange(
-        field, wet, forward, spectral_weight, lats, zs, xs, 1.0 / math.sqrt(total_lon)
+    mixed, edged, wets, inverse = exchange(
+        field, ocean, modes, spectral_weight, lats, zs, xs, 1.0 / math.sqrt(total_lon)
     )
-    lon_ids = (lon_start - PAD + jnp.arange(width + 2 * PAD, dtype=jnp.int32) + total_lon) % total_lon
-    inverse = jnp.concatenate(stored_halves(table_of(lon_ids[:, None], pair[None], parity[None], total_lon)), 1)
     mixed = mixed.reshape(2, 2 * total_modes, -1)
     return tail(
         mixed, edged, wets, inverse, local_weight, layer_bias,

time: 87.7 us -> 71.5 us (0.82)
  Pallas kernels: 82 us -> 71.4 us
  other arithmetic: 3.15 us -> 0 us
  local copies, waits for them, and re-layouts: 2.03 us -> 0.02 us
    pallas_call x1, Pallas kernels: 64.4 us -> 57.6 us  [exchange(): pl.pallas_call(functools.partial(exchange_kernel, zs, xs, lats, scale), o...]
    pallas_call x1, Pallas kernels: 17.6 us -> 13.7 us  [tail(): pl.pallas_call(functools.partial(tail_kernel, rows, width, scale, lat_axi...]
    convert_element_type x3 -> x0, other arithmetic: 3.09 us -> none  [the longest x2 2.23 us: stored_halves(): return (high.astype(BF), (value - high).astype(BF))]
    unnamed x12 -> x8, local copies, waits for them, and re-layouts: 0.96 us -> 0.02 us
where the time goes in v2:
time: 71.5 us; the launch traced here: 71.4 us
  Pallas kernels  71.4 us (100%)
    pallas_call x1, Pallas kernels, exchange(): pl.pallas_call(functools.partial(exchange_kernel, zs, xs, lats, scale), o...  57.6 us
    pallas_call x1, Pallas kernels, tail(): pl.pallas_call(functools.partial(tail_kernel, rows, width, scale, lat_axi...  13.7 us

profile of v2, /device:TPU:1, one launch (start us, length us, event | category | flops | bytes accessed | tf_op | source)
XLA Modules:
  0.0 71.4 jit_solution(15502262923048953268)
XLA Ops:
  0.0 0.0 copy-start.3
  0.0 0.0 copy-start
  0.0 0.0 copy-start.2
  0.0 0.0 copy-start.1
  0.0 57.6 %exchange.1 = (f32[2,8,4,8,1152]{4,3,2,1,0:T(8,128)S(1)}, f32[18,272,128]{2,1,0:T(8,128)S(1)}, f32[3,272,128]{2,1,0:T(8,128)S(1)}, bf16[272,512]{1,0:T(8,128)(2,1)S(1)}) custom-call(f32[16,256,128]{2,1,0:T(8,128)} %field_hbm.1, s32[16,256]{1,0:T(8,128)} %ocean_hbm.1, s32[1,128]{1,0:T(1,128)} %bitcast.7, f32[2,2,128,128]{3,2,1,0:T(8,128)} %weight_hbm.1), custom_call_target="tpu_custom_call" | custom-call | tf_op jit(solution)/shard_map/exchange/pallas_call | solution.py:413
  57.7 0.0 copy-done.3
  57.7 0.0 copy-done
  57.7 0.0 copy-done.2
  57.7 0.0 copy-done.1
  57.7 13.7 %tail.1 = f32[16,256,128]{2,1,0:T(8,128)} custom-call(f32[2,256,1152]{2,1,0:T(8,128)S(1)} %bitcast.4, f32[18,272,128]{2,1,0:T(8,128)S(1)} %get-tuple-element.10.field, f32[3,272,128]{2,1,0:T(8,128)S(1)} %get-tuple-element.11.wet_ref, bf16[272,512]{1,0:T(8,128)(2,1)S(1)} %get-tuple-element.12.table_ref, f32[128,128]{1,0:T(8,128)S(1)} %copy-done.1, ...), custom_call_target="tpu_custom_call" | custom-call | tf_op jit(solution)/shard_map/tail/pallas_call | solution.py:111
Async XLA Ops:
  0.0 57.7 %copy-start.3 = (f32[128]{0:T(128)S(1)}, f32[128]{0:T(128)}, u32[]{:S(2)}) copy-start(f32[128]{0:T(128)} %param.15) | copy-start | bytes 1540
  0.0 57.7 %copy-start = (f32[3,3,128,128]{3,2,1,0:T(8,128)S(1)}, f32[3,3,128,128]{3,2,1,0:T(8,128)}, u32[]{:S(2)}) copy-start(f32[3,3,128,128]{3,2,1,0:T(8,128)} %conv_ref.1) | copy-start | bytes 1769476
  0.0 57.7 %copy-start.2 = (f32[128]{0:T(128)S(1)}, f32[128]{0:T(128)}, u32[]{:S(2)}) copy-start(f32[128]{0:T(128)} %param.13) | copy-start | bytes 1540
  0.0 57.7 %copy-start.1 = (f32[128,128]{1,0:T(8,128)S(1)}, f32[128,128]{1,0:T(8,128)}, u32[]{:S(2)}) copy-start(f32[128,128]{1,0:T(8,128)} %local_ref.1) | copy-start | bytes 196612

commit v3 on v2

--- a/solution.py
+++ b/solution.py
@@ -59,7 +59,7 @@
     bottom = pltpu.roll(wet_ref[2], rows, 1) * below
     wet = jnp.where(lane == 0, top, jnp.where(lane == rows + 1, bottom, wet_ref[1])).astype(BF)
 
-    @pl.loop(0, ext)
+    @pl.loop(0, ext, unroll=3)
     def _(r):
         outer = (r == 0) | (r == ext - 1)
         second = (r > half) & (r < ext - 1) | (r == 0)
@@ -81,7 +81,7 @@
 
     group = 2
 
-    @pl.loop(0, rows // group)
+    @pl.loop(0, rows // group, unroll=2)
     def _(t):
         i = t * group
         block = hidden[pl.ds(i + 2, group)].reshape(group * wide, 768)
@@ -213,20 +213,35 @@
         pending.append(copy)
         return copy
 
-    def coefficients(first):
-        pltpu.make_async_copy(field_hbm.at[0], field.at[0], load_sem.at[first]).wait()
-        pltpu.make_async_copy(field_hbm.at[0], field.at[0], load_sem.at[first + 1]).wait()
+    order = (4, 3, 5, 2, 6, 1, 7, 0)
+    slices = [wrap(z + step, zs) for step in order]
+    each = xs * 8
+    group = 4 * each
+
+    def loaded(first):
+        for row in (first, first + 1):
+            pltpu.make_async_copy(field_hbm.at[0], field.at[0], load_sem.at[row]).wait()
+
+    def coefficients(first, g):
+        waves = jnp.concatenate([
+            table[pl.ds(pl.multiple_of(zz * each, each), each)] for zz in slices[4 * g : 4 * g + 4]
+        ], 0)
         high, low = halves(jnp.concatenate([field[first], field[first + 1]], 1))
-        result = dot(table[...], jnp.concatenate([high, high], 0)) + dot(table[:, :width], low)
+        result = dot(waves, jnp.concatenate([high, high], 0)) + dot(waves[:, :width], low)
         return result * scale
 
     pairs = half // 2
     pair_copies = []
-    for p in range(pairs):
-        sent[p] = coefficients(other * half + 2 * p)
-        if p == 0:
-            pl.semaphore_wait(barrier, len(friends))
-        pair_copies.append(send(sent.at[p], got.at[p], pair_sem, p, device(core=other)))
+    for g in range(2):
+        for p in range(pairs):
+            if g == 0:
+                loaded(other * half + 2 * p)
+            sent[g, p] = coefficients(other * half + 2 * p, g)
+            if g == 0 and p == 0:
+                pl.semaphore_wait(barrier, len(friends))
+            pair_copies.append(
+                send(sent.at[g, p], got.at[g, p], pair_sem, len(pair_copies), device(core=other))
+            )
     weight_copy = send(weight_hbm, weight.at[core], halo_sem, 1, device(core=other))
 
     edges = []
@@ -239,12 +254,21 @@
     edge(wet, wets.at[0, pl.ds(PAD, width)], device(lat=south))
     edge(wet, wets.at[2, pl.ds(PAD, width)], device(lat=north))
 
-    for p in range(pairs):
-        mine = coefficients(core * half + 2 * p)
-        pair_copies[p].wait_recv()
-        mine = mine + got[p]
-        sums[:, :, :, pl.ds(p * 256, 256)] = mine.reshape(zs, xs, 8, 256)
-
+    low_lanes, high_lanes = pl.ds(0, cut), pl.ds(cut, cut)
+    firsts = []
+    for g in range(2):
+        for p in range(pairs):
+            if g == 0:
+                loaded(core * half + 2 * p)
+            mine = coefficients(core * half + 2 * p, g)
+            pair_copies[g * pairs + p].wait_recv()
+            mine = mine + got[g, p]
+            sums[pl.ds(4 * g, 4), :, :, pl.ds(p * 256, 256)] = mine.reshape(4, xs, 8, 256)
+        for n in range(4 * g, 4 * g + 4):
+            firsts.append((
+                send(sums.at[n, across, :, low_lanes], half_a.at[n], x_sem, n, device(x=right)),
+                send(sums.at[n, across, :, high_lanes], half_b.at[n], x_sem, 8 + n, device(x=left)),
+            ))
     middle = pl.ds(PAD, width)
     inner = [
         pltpu.make_async_copy(field, edged.at[pl.ds(1, rows), middle], local_sem.at[1]),
@@ -254,23 +278,14 @@
     for copy in inner + [kept_table]:
         copy.start()
 
-    order = (4, 3, 5, 2, 6, 1, 7, 0)
-    slices = [wrap(z + step, zs) for step in order]
-    low_lanes, high_lanes = pl.ds(0, cut), pl.ds(cut, cut)
-    firsts = []
-    for n, zz in enumerate(slices):
-        firsts.append((
-            send(sums.at[zz, across, :, low_lanes], half_a.at[n], x_sem, n, device(x=right)),
-            send(sums.at[zz, across, :, high_lanes], half_b.at[n], x_sem, 8 + n, device(x=left)),
-        ))
     seconds = []
-    for n, zz in enumerate(slices):
+    for n in range(len(slices)):
         firsts[n][0].wait_recv()
-        sums[zz, right, :, low_lanes] = sums[zz, right, :, low_lanes] + half_a[n]
-        to_right = send(sums.at[zz, right], full_a.at[n], x_sem, 16 + n, device(x=right))
+        sums[n, right, :, low_lanes] = sums[n, right, :, low_lanes] + half_a[n]
+        to_right = send(sums.at[n, right], full_a.at[n], x_sem, 16 + n, device(x=right))
         firsts[n][1].wait_recv()
-        sums[zz, left, :, high_lanes] = sums[zz, left, :, high_lanes] + half_b[n]
-        to_left = send(sums.at[zz, left], full_b.at[n], x_sem, 24 + n, device(x=left))
+        sums[n, left, :, high_lanes] = sums[n, left, :, high_lanes] + half_b[n]
+        to_left = send(sums.at[n, left], full_b.at[n], x_sem, 24 + n, device(x=left))
         seconds.append((to_right, to_left))
 
     def send_edges():
@@ -283,33 +298,34 @@
             edge(wets.at[:, pl.ds(source, PAD)], wets.at[:, pl.ds(target, PAD)], device(**lon))
 
     rising, falling = [], []
-    for n, zz in enumerate(slices):
+    for n in range(len(slices)):
         seconds[n][0].wait_recv()
         seconds[n][1].wait_recv()
-        total = sums[zz, x] + full_a[n] + full_b[n]
-        step = (n - 1) // 2
+        total = sums[n, x] + full_a[n] + full_b[n]
         if n == 0:
             part[n] = total
-            rising.append(send(part.at[n, :, low_lanes], up.at[0, :, low_lanes], z_sem, 0, device(z=higher)))
-            falling.append(send(part.at[n, :, high_lanes], down.at[0, :, high_lanes], z_sem, 4, device(z=lower)))
+            rising.append(send(part.at[n, :, low_lanes], up.at[0, :, low_lanes], z_sem, 0, device(z=beyond)))
+            falling.append(send(part.at[n, :, high_lanes], down.at[0, :, high_lanes], z_sem, 4, device(z=behind)))
             send_edges()
         elif n == 7:
-            rising[3].wait_recv()
-            falling[3].wait_recv()
-            total = total + up[3] + down[3]
+            for buffer, chain in ((up, rising), (down, falling)):
+                for hop in (2, 3):
+                    chain[hop].wait_recv()
+                    total = total + buffer[hop]
         else:
             rises = n % 2 == 1
-            chain, buffer = (rising, up) if rises else (falling, down)
-            chain[step].wait_recv()
-            if step == 0:
-                span = low_lanes if rises else high_lanes
-                part[n] = total
+            hop = (n + 1) // 2
+            chain, buffer, span = (rising, up, low_lanes) if rises else (falling, down, high_lanes)
+            near, far = (higher, beyond) if rises else (lower, behind)
+            part[n] = total
+            if hop == 2:
+                chain[0].wait_recv()
+                chain[1].wait_recv()
+                part[n] = part[n] + buffer[1]
                 part[n, :, span] = part[n, :, span] + buffer[0, :, span]
-            else:
-                part[n] = total + buffer[step]
             chain.append(send(
-                part.at[n], buffer.at[step + 1], z_sem, (0 if rises else 4) + step + 1,
-                device(z=higher if rises else lower),
+                part.at[n], buffer.at[hop], z_sem, (0 if rises else 4) + hop,
+                device(z=far if hop == 2 else near),
             ))
 
     own_weight.wait()
@@ -428,8 +444,8 @@
             pltpu.VMEM((wide, 512), BF),
             pltpu.VMEM((rows, width, 128), F32),
             pltpu.VMEM((2, *weight.shape), F32),
-            pltpu.VMEM((rows // 4, 256, 256), F32),
-            pltpu.VMEM((rows // 4, 256, 256), F32),
+            pltpu.VMEM((2, rows // 4, 128, 256), F32),
+            pltpu.VMEM((2, rows // 4, 128, 256), F32),
             pltpu.VMEM((zs, xs, 8, lanes), F32),
             pltpu.VMEM((zs, 8, lanes // 2), F32),
             pltpu.VMEM((zs, 8, lanes // 2), F32),
@@ -440,7 +456,7 @@
             pltpu.VMEM((4, 8, lanes), F32),
             pltpu.VMEM((8, 128), F32),
             pltpu.VMEM((zs, xs, 8, lanes + 128), F32),
-            dma((rows,)), dma((2, 4)), dma((2, 32)), dma((2, 8)), dma((2, 2)), dma((2, 8)),
+            dma((rows,)), dma((2, 8)), dma((2, 32)), dma((2, 8)), dma((2, 2)), dma((2, 8)),
             dma((2, 32)), dma((2, 8)), dma((2, 8)), dma((14,)),
         ],
         compiler_params=pltpu.CompilerParams(

time: 71.5 us -> 64.3 us (0.90)
  Pallas kernels: 71.4 us -> 64.2 us
    pallas_call x1, Pallas kernels: 57.6 us -> 53.4 us  [exchange(): pl.pallas_call(functools.partial(exchange_kernel, zs, xs, lats, scale), o...]
    pallas_call x1, Pallas kernels: 13.7 us -> 10.7 us  [tail(): pl.pallas_call(functools.partial(tail_kernel, rows, width, scale, lat_axi...]
where the time goes in v3:
time: 64.3 us; the launch traced here: 64.2 us
  Pallas kernels  64.2 us (100%)
    pallas_call x1, Pallas kernels, exchange(): pl.pallas_call(functools.partial(exchange_kernel, zs, xs, lats, scale), o...  53.4 us
    pallas_call x1, Pallas kernels, tail(): pl.pallas_call(functools.partial(tail_kernel, rows, width, scale, lat_axi...  10.7 us

profile of v3, /device:TPU:1, one launch (start us, length us, event | category | flops | bytes accessed | tf_op | source)
XLA Modules:
  0.0 64.2 jit_solution(12111101298580733304)
XLA Ops:
  0.0 0.0 copy-start.3
  0.0 0.0 copy-start
  0.0 0.0 copy-start.2
  0.0 0.0 copy-start.1
  0.0 53.4 %exchange.1 = (f32[2,8,4,8,1152]{4,3,2,1,0:T(8,128)S(1)}, f32[18,272,128]{2,1,0:T(8,128)S(1)}, f32[3,272,128]{2,1,0:T(8,128)S(1)}, bf16[272,512]{1,0:T(8,128)(2,1)S(1)}) custom-call(f32[16,256,128]{2,1,0:T(8,128)} %field_hbm.1, s32[16,256]{1,0:T(8,128)} %ocean_hbm.1, s32[1,128]{1,0:T(1,128)} %bitcast.7, f32[2,2,128,128]{3,2,1,0:T(8,128)} %weight_hbm.1), custom_call_target="tpu_custom_call" | custom-call | tf_op jit(solution)/shard_map/exchange/pallas_call | solution.py:429
  53.4 0.0 copy-done.3
  53.5 0.0 copy-done
  53.5 0.0 copy-done.2
  53.5 0.0 copy-done.1
  53.5 10.7 %tail.1 = f32[16,256,128]{2,1,0:T(8,128)} custom-call(f32[2,256,1152]{2,1,0:T(8,128)S(1)} %bitcast.4, f32[18,272,128]{2,1,0:T(8,128)S(1)} %get-tuple-element.10.field, f32[3,272,128]{2,1,0:T(8,128)S(1)} %get-tuple-element.11.wet_ref, bf16[272,512]{1,0:T(8,128)(2,1)S(1)} %get-tuple-element.12.table_ref, f32[128,128]{1,0:T(8,128)S(1)} %copy-done.1, ...), custom_call_target="tpu_custom_call" | custom-call | tf_op jit(solution)/shard_map/tail/pallas_call | solution.py:111
Async XLA Ops:
  0.0 53.4 %copy-start.3 = (f32[128]{0:T(128)S(1)}, f32[128]{0:T(128)}, u32[]{:S(2)}) copy-start(f32[128]{0:T(128)} %param.15) | copy-start | bytes 1540
  0.0 53.5 %copy-start = (f32[3,3,128,128]{3,2,1,0:T(8,128)S(1)}, f32[3,3,128,128]{3,2,1,0:T(8,128)}, u32[]{:S(2)}) copy-start(f32[3,3,128,128]{3,2,1,0:T(8,128)} %conv_ref.1) | copy-start | bytes 1769476
  0.0 53.5 %copy-start.2 = (f32[128]{0:T(128)S(1)}, f32[128]{0:T(128)}, u32[]{:S(2)}) copy-start(f32[128]{0:T(128)} %param.13) | copy-start | bytes 1540
  0.0 53.5 %copy-start.1 = (f32[128,128]{1,0:T(8,128)S(1)}, f32[128,128]{1,0:T(8,128)}, u32[]{:S(2)}) copy-start(f32[128,128]{1,0:T(8,128)} %local_ref.1) | copy-start | bytes 196612

commit v4 on v3

--- a/solution.py
+++ b/solution.py
@@ -59,7 +59,7 @@
     bottom = pltpu.roll(wet_ref[2], rows, 1) * below
     wet = jnp.where(lane == 0, top, jnp.where(lane == rows + 1, bottom, wet_ref[1])).astype(BF)
 
-    @pl.loop(0, ext, unroll=3)
+    @pl.loop(0, ext, unroll=6)
     def _(r):
         outer = (r == 0) | (r == ext - 1)
         second = (r > half) & (r < ext - 1) | (r == 0)
@@ -79,9 +79,9 @@
         for a in range(3):
             hidden[r + 2 - a, :, pl.ds(a * 256, 256)] = both
 
-    group = 2
-
-    @pl.loop(0, rows // group, unroll=2)
+    group = 4
+
+    @pl.loop(0, rows // group, unroll=4)
     def _(t):
         i = t * group
         block = hidden[pl.ds(i + 2, group)].reshape(group * wide, 768)
@@ -341,32 +341,35 @@
     even = lax.rem(spot, 2) == 0
     mixed = real + jnp.where(even, -pltpu.roll(imag, half * 8 - 1, 0), pltpu.roll(imag, 1, 0))
     for i in range(half):
-        whole[z, x, :, pl.ds(i * 128, 128)] = mixed[i * 8 : (i + 1) * 8]
+        whole[:, pl.ds(i * 128, 128)] = mixed[i * 8 : (i + 1) * 8]
     halo[...] = jnp.where(core == 0, mixed[:8], mixed[(half - 1) * 8 :])
     tail_lanes = pl.ds(lanes, 128)
-    row_copy = send(halo, whole.at[z, x, :, tail_lanes], halo_sem, 0, device(lat=wrap(lat - 1 + 2 * core, lats)))
+    row_copy = send(halo, whole.at[:, tail_lanes], halo_sem, 0, device(lat=wrap(lat - 1 + 2 * core, lats)))
     row_copy.wait_recv()
+    kept = pltpu.make_async_copy(whole, mixed_out.at[core, z, x], local_sem.at[3])
+    kept.start()
 
     front, back = pl.ds(0, cut), pl.ds(cut, lanes + 128 - cut)
     order = (0, 7, 1, 6, 2, 5, 3, 4)
     slices = [wrap(z + step, zs) for step in order]
-    sideways, relays, locals_, gathered = [], [], [], []
+    sideways, relays, gathered = [], [], []
 
     def spread(n):
         zz = slices[n]
-        mine = whole.at[zz, x]
+        mine = mixed_out.at[core, zz, x]
+        source = whole if n == 0 else mine
         sideways.append((
-            send(mine, mine, gx_sem, n, device(x=right)),
-            send(mine, mine, gx_sem, 8 + n, device(x=left)),
+            send(source, mine, gx_sem, n, device(x=right)),
+            send(source, mine, gx_sem, 8 + n, device(x=left)),
         ))
 
     def relay(n):
         zz = slices[n]
         sideways[n][0].wait_recv()
-        from_left = whole.at[zz, left, :, front]
+        from_left = mixed_out.at[core, zz, left, :, front]
         first = send(from_left, from_left, gx_sem, 16 + n, device(x=right))
         sideways[n][1].wait_recv()
-        from_right = whole.at[zz, right, :, back]
+        from_right = mixed_out.at[core, zz, right, :, back]
         second = send(from_right, from_right, gx_sem, 24 + n, device(x=left))
         relays.append((first, second))
 
@@ -374,14 +377,16 @@
         zz = slices[n]
         relays[n][0].wait_recv()
         relays[n][1].wait_recv()
-        gathered.append(send(whole.at[zz], mixed_out.at[core, zz], gp_sem, n, device(core=other)))
-        kept = pltpu.make_async_copy(whole.at[zz], mixed_out.at[core, zz], local_sem.at[3 + n])
-        kept.start()
-        locals_.append(kept)
+        if n == 0:
+            kept.wait()
+        done = mixed_out.at[core, zz]
+        gathered.append(send(done, done, gp_sem, n, device(core=other)))
 
     def along(n, where, index, span=None):
-        source = whole.at[slices[n], x] if span is None else whole.at[slices[n], x, :, span]
-        return send(source, source, gz_sem, index, device(z=where))
+        spot = mixed_out.at[core, slices[n], x]
+        if span is not None:
+            spot = mixed_out.at[core, slices[n], x, :, span]
+        return send(whole if n == 0 else spot, spot, gz_sem, index, device(z=where))
 
     far_up, far_down = along(0, beyond, 2), along(0, behind, 3)
     near_up, near_down = along(0, higher, 0), along(0, lower, 1)
@@ -391,9 +396,11 @@
     near_down.wait_recv()
     spread(2)
     far_up.wait_recv()
-    next_up, half_up = along(3, higher, 4), along(3, beyond, 6, front)
+    next_up = along(3, higher, 4)
+    half_up = along(3, beyond, 6, front)
     far_down.wait_recv()
-    next_down, half_down = along(4, lower, 5), along(4, behind, 7, back)
+    next_down = along(4, lower, 5)
+    half_down = along(4, behind, 7, back)
     spread(3)
     spread(4)
     for n in range(3):
@@ -402,22 +409,27 @@
     spread(5)
     next_down.wait_recv()
     spread(6)
+    relay(3)
+    relay(4)
+    finish(0)
     half_up.wait_recv()
     half_down.wait_recv()
     spread(7)
-    finish(0)
-    for n in range(3, 8):
-        relay(n)
-        finish(n - 2)
-    finish(6)
-    finish(7)
+    relay(5)
+    finish(1)
+    finish(2)
+    relay(6)
+    finish(3)
+    finish(4)
+    relay(7)
+    for n in range(5, 8):
+        finish(n)
 
     for copy in edges[4:] + gathered:
         copy.wait_recv()
     for copy in pending:
         copy.wait_send()
-    for copy in locals_ + [kept_table]:
-        copy.wait()
+    kept_table.wait()
 
 
 def exchange(field, ocean, modes, weight, lats, zs, xs, scale):
@@ -455,7 +467,7 @@
             pltpu.VMEM((4, 8, lanes), F32),
             pltpu.VMEM((4, 8, lanes), F32),
             pltpu.VMEM((8, 128), F32),
-            pltpu.VMEM((zs, xs, 8, lanes + 128), F32),
+            pltpu.VMEM((8, lanes + 128), F32),
             dma((rows,)), dma((2, 8)), dma((2, 32)), dma((2, 8)), dma((2, 2)), dma((2, 8)),
             dma((2, 32)), dma((2, 8)), dma((2, 8)), dma((14,)),
         ],

time: 64.3 us -> 62.9 us (0.978)
  Pallas kernels: 64.2 us -> 62.7 us
    pallas_call x1, Pallas kernels: 10.7 us -> 9.68 us  [tail(): pl.pallas_call(functools.partial(tail_kernel, rows, width, scale, lat_axi...]
where the time goes in v4:
time: 62.9 us; the launch traced here: 62.8 us
  Pallas kernels  62.7 us (100%)
    pallas_call x1, Pallas kernels, exchange(): pl.pallas_call(functools.partial(exchange_kernel, zs, xs, lats, scale), o...  53 us
    pallas_call x1, Pallas kernels, tail(): pl.pallas_call(functools.partial(tail_kernel, rows, width, scale, lat_axi...  9.68 us

profile of v4, /device:TPU:1, one launch (start us, length us, event | category | flops | bytes accessed | tf_op | source)
XLA Modules:
  0.0 62.8 jit_solution(6807278810146982108)
XLA Ops:
  0.0 0.0 copy-start.3
  0.0 0.0 copy-start
  0.0 0.0 copy-start.2
  0.0 0.0 copy-start.1
  0.0 53.0 %exchange.1 = (f32[2,8,4,8,1152]{4,3,2,1,0:T(8,128)S(1)}, f32[18,272,128]{2,1,0:T(8,128)S(1)}, f32[3,272,128]{2,1,0:T(8,128)S(1)}, bf16[272,512]{1,0:T(8,128)(2,1)S(1)}) custom-call(f32[16,256,128]{2,1,0:T(8,128)} %field_hbm.1, s32[16,256]{1,0:T(8,128)} %ocean_hbm.1, s32[1,128]{1,0:T(1,128)} %bitcast.7, f32[2,2,128,128]{3,2,1,0:T(8,128)} %weight_hbm.1), custom_call_target="tpu_custom_call" | custom-call | tf_op jit(solution)/shard_map/exchange/pallas_call | solution.py:441
  53.1 0.0 copy-done.3
  53.1 0.0 copy-done
  53.1 0.0 copy-done.2
  53.1 0.0 copy-done.1
  53.1 9.7 %tail.1 = f32[16,256,128]{2,1,0:T(8,128)} custom-call(f32[2,256,1152]{2,1,0:T(8,128)S(1)} %bitcast.4, f32[18,272,128]{2,1,0:T(8,128)S(1)} %get-tuple-element.10.field, f32[3,272,128]{2,1,0:T(8,128)S(1)} %get-tuple-element.11.wet_ref, bf16[272,512]{1,0:T(8,128)(2,1)S(1)} %get-tuple-element.12.table_ref, f32[128,128]{1,0:T(8,128)S(1)} %copy-done.1, ...), custom_call_target="tpu_custom_call" | custom-call | tf_op jit(solution)/shard_map/tail/pallas_call | solution.py:111
Async XLA Ops:
  0.0 53.1 %copy-start.3 = (f32[128]{0:T(128)S(1)}, f32[128]{0:T(128)}, u32[]{:S(2)}) copy-start(f32[128]{0:T(128)} %param.15) | copy-start | bytes 1540
  0.0 53.1 %copy-start = (f32[3,3,128,128]{3,2,1,0:T(8,128)S(1)}, f32[3,3,128,128]{3,2,1,0:T(8,128)}, u32[]{:S(2)}) copy-start(f32[3,3,128,128]{3,2,1,0:T(8,128)} %conv_ref.1) | copy-start | bytes 1769476
  0.0 53.1 %copy-start.2 = (f32[128]{0:T(128)S(1)}, f32[128]{0:T(128)}, u32[]{:S(2)}) copy-start(f32[128]{0:T(128)} %param.13) | copy-start | bytes 1540
  0.0 53.1 %copy-start.1 = (f32[128,128]{1,0:T(8,128)S(1)}, f32[128,128]{1,0:T(8,128)}, u32[]{:S(2)}) copy-start(f32[128,128]{1,0:T(8,128)} %local_ref.1) | copy-start | bytes 196612

commit v5 on v4

--- a/solution.py
+++ b/solution.py
@@ -345,9 +345,7 @@
     halo[...] = jnp.where(core == 0, mixed[:8], mixed[(half - 1) * 8 :])
     tail_lanes = pl.ds(lanes, 128)
     row_copy = send(halo, whole.at[:, tail_lanes], halo_sem, 0, device(lat=wrap(lat - 1 + 2 * core, lats)))
-    row_copy.wait_recv()
     kept = pltpu.make_async_copy(whole, mixed_out.at[core, z, x], local_sem.at[3])
-    kept.start()
 
     front, back = pl.ds(0, cut), pl.ds(cut, lanes + 128 - cut)
     order = (0, 7, 1, 6, 2, 5, 3, 4)
@@ -386,19 +384,26 @@
         spot = mixed_out.at[core, slices[n], x]
         if span is not None:
             spot = mixed_out.at[core, slices[n], x, :, span]
-        return send(whole if n == 0 else spot, spot, gz_sem, index, device(z=where))
-
-    far_up, far_down = along(0, beyond, 2), along(0, behind, 3)
-    near_up, near_down = along(0, higher, 0), along(0, lower, 1)
+        return send(whole.at[:, span] if n == 0 else spot, spot, gz_sem, index, device(z=where))
+
+    paths = (beyond, behind, higher, lower)
+    own = [along(0, where, index, pl.ds(0, lanes)) for index, where in enumerate(paths)]
+    row_copy.wait_recv()
+    kept.start()
+    added = [along(0, where, 8 + index, tail_lanes) for index, where in enumerate(paths)]
     spread(0)
-    near_up.wait_recv()
+    own[2].wait_recv()
+    added[2].wait_recv()
     spread(1)
-    near_down.wait_recv()
+    own[3].wait_recv()
+    added[3].wait_recv()
     spread(2)
-    far_up.wait_recv()
+    own[0].wait_recv()
+    added[0].wait_recv()
     next_up = along(3, higher, 4)
     half_up = along(3, beyond, 6, front)
-    far_down.wait_recv()
+    own[1].wait_recv()
+    added[1].wait_recv()
     next_down = along(4, lower, 5)
     half_down = along(4, behind, 7, back)
     spread(3)
@@ -468,7 +473,7 @@
             pltpu.VMEM((4, 8, lanes), F32),
             pltpu.VMEM((8, 128), F32),
             pltpu.VMEM((8, lanes + 128), F32),
-            dma((rows,)), dma((2, 8)), dma((2, 32)), dma((2, 8)), dma((2, 2)), dma((2, 8)),
+            dma((rows,)), dma((2, 8)), dma((2, 32)), dma((2, 8)), dma((2, 2)), dma((2, 12)),
             dma((2, 32)), dma((2, 8)), dma((2, 8)), dma((14,)),
         ],
         compiler_params=pltpu.CompilerParams(

time: 62.9 us -> 61.5 us (0.978)
  Pallas kernels: 62.7 us -> 61.3 us
    pallas_call x1, Pallas kernels: 53 us -> 51.6 us  [exchange(): pl.pallas_call(functools.partial(exchange_kernel, zs, xs, lats, scale), o...]
where the time goes in v5:
time: 61.5 us; the launch traced here: 61.4 us
  Pallas kernels  61.3 us (100%)
    pallas_call x1, Pallas kernels, exchange(): pl.pallas_call(functools.partial(exchange_kernel, zs, xs, lats, scale), o...  51.6 us
    pallas_call x1, Pallas kernels, tail(): pl.pallas_call(functools.partial(tail_kernel, rows, width, scale, lat_axi...  9.68 us

profile of v5, /device:TPU:1, one launch (start us, length us, event | category | flops | bytes accessed | tf_op | source)
XLA Modules:
  0.0 61.4 jit_solution(10194188645321900851)
XLA Ops:
  0.0 0.0 copy-start.3
  0.0 0.0 copy-start
  0.0 0.0 copy-start.2
  0.0 0.0 copy-start.1
  0.0 51.6 %exchange.1 = (f32[2,8,4,8,1152]{4,3,2,1,0:T(8,128)S(1)}, f32[18,272,128]{2,1,0:T(8,128)S(1)}, f32[3,272,128]{2,1,0:T(8,128)S(1)}, bf16[272,512]{1,0:T(8,128)(2,1)S(1)}) custom-call(f32[16,256,128]{2,1,0:T(8,128)} %field_hbm.1, s32[16,256]{1,0:T(8,128)} %ocean_hbm.1, s32[1,128]{1,0:T(1,128)} %bitcast.7, f32[2,2,128,128]{3,2,1,0:T(8,128)} %weight_hbm.1), custom_call_target="tpu_custom_call" | custom-call | tf_op jit(solution)/shard_map/exchange/pallas_call | solution.py:446
  51.6 0.0 copy-done.3
  51.7 0.0 copy-done
  51.7 0.0 copy-done.2
  51.7 0.0 copy-done.1
  51.7 9.7 %tail.1 = f32[16,256,128]{2,1,0:T(8,128)} custom-call(f32[2,256,1152]{2,1,0:T(8,128)S(1)} %bitcast.4, f32[18,272,128]{2,1,0:T(8,128)S(1)} %get-tuple-element.10.field, f32[3,272,128]{2,1,0:T(8,128)S(1)} %get-tuple-element.11.wet_ref, bf16[272,512]{1,0:T(8,128)(2,1)S(1)} %get-tuple-element.12.table_ref, f32[128,128]{1,0:T(8,128)S(1)} %copy-done.1, ...), custom_call_target="tpu_custom_call" | custom-call | tf_op jit(solution)/shard_map/tail/pallas_call | solution.py:111
Async XLA Ops:
  0.0 51.6 %copy-start.3 = (f32[128]{0:T(128)S(1)}, f32[128]{0:T(128)}, u32[]{:S(2)}) copy-start(f32[128]{0:T(128)} %param.15) | copy-start | bytes 1540
  0.0 51.7 %copy-start = (f32[3,3,128,128]{3,2,1,0:T(8,128)S(1)}, f32[3,3,128,128]{3,2,1,0:T(8,128)}, u32[]{:S(2)}) copy-start(f32[3,3,128,128]{3,2,1,0:T(8,128)} %conv_ref.1) | copy-start | bytes 1769476
  0.0 51.7 %copy-start.2 = (f32[128]{0:T(128)S(1)}, f32[128]{0:T(128)}, u32[]{:S(2)}) copy-start(f32[128]{0:T(128)} %param.13) | copy-start | bytes 1540
  0.0 51.7 %copy-start.1 = (f32[128,128]{1,0:T(8,128)S(1)}, f32[128,128]{1,0:T(8,128)}, u32[]{:S(2)}) copy-start(f32[128,128]{1,0:T(8,128)} %local_ref.1) | copy-start | bytes 196612
